TPU v7x, 32 devices: a whole 2x2x4 slice. The times are simulated.
32 devices in a mesh: gx: 4 (over y, x), gy: 4 (over z), gz: 2 (over core).
Axes of the slice: x: 2, y: 2, z: 4, core: 2. Of those that a mesh axis runs over, the one named last changes fastest.
Arguments:
- particles: float32 [32, 32, 16, 128], P('gx', 'gy', 'gz'), may hold values from -6 to 6, as said below
- counts: int32 [32, 32, 16], P('gx', 'gy', 'gz'), may hold values from 1 to 32, as said below
Outputs:
- potential: float32 [32, 32, 512], P('gx', 'gy', 'gz')
- near_potential: float32 [32, 32, 512], P('gx', 'gy', 'gz')
Inputs may be any that keep to these rules, and one draw needn't show every extreme that they name: `particles`: in each leaf the first 96 entries are offsets from the leaf's centre in leaf sides, three blocks of 32 for the three coordinates, within -0.5 and 0.5; the last 32 are strengths. `counts`: slots from the count on are padding; some leaf is full.
All inputs are finite; a program needn't handle non-finite values.
Results may differ from a plain program's by a relative error of at most 0.0003.
Values sent between devices are 32-bit elements; how exact they have to be, the bound alone decides.
A program may use at most 64 MiB of HBM per device.

v0:
```python
import math

import jax
import jax.numpy as jnp
from jax import lax
from jax.sharding import PartitionSpec as P

Q = 64


INV_FOUR_PI = 0.07957747154594767
INNER = 0.9
OUTER = 1.5
PARENT_CHECK = 3.0
SOFTEN_SQUARED = 0.0625
REGULAR = 0.01
HIGHEST = lax.Precision.HIGHEST
far_block = 32


def extended(cells, sides, width):
    for axis, dim in sides:
        count = lax.axis_size(axis)
        ends = count - 1
        head = lax.slice_in_dim(cells, 0, width, axis=dim)
        tail = lax.slice_in_dim(cells, cells.shape[dim] - width, cells.shape[dim], axis=dim)
        cells = jnp.concatenate(
            [
                lax.ppermute(tail, axis, [(i, (i + 1) % count) for i in range(ends)]),
                cells,
                lax.ppermute(head, axis, [((i + 1) % count, i) for i in range(ends)]),
            ],
            axis=dim,
        )
    return cells


def sphere(number):
    order = jnp.arange(number, dtype=jnp.float32)
    height = 1.0 - (2.0 * order + 1.0) / number
    radial = jnp.sqrt(1.0 - height * height)
    turning = order * (math.pi * (3.0 - math.sqrt(5.0)))
    return jnp.stack([radial * jnp.cos(turning), radial * jnp.sin(turning), height])


def green(first, second, third):
    return INV_FOUR_PI / jnp.sqrt(first * first + second * second + third * third)


def factor_lower(normal):
    number = normal.shape[0]
    rows = jnp.arange(number, dtype=jnp.int32)

    def column_turn(column, factor):
        column = column.astype(jnp.int32)
        select = (rows == column).astype(jnp.float32)
        own_row = jnp.dot(select, factor, precision=HIGHEST)
        residue = jnp.dot(normal, select, precision=HIGHEST) - jnp.dot(
            factor, own_row, precision=HIGHEST
        )
        pivot = jnp.sqrt(jnp.dot(select, residue, precision=HIGHEST))
        newcol = jnp.where(rows >= column, residue / pivot, 0.0)
        return factor + newcol[:, None] * select[None, :]

    return lax.fori_loop(0, number, column_turn, jnp.zeros_like(normal))


def solve_lower(factor, right):
    number = factor.shape[0]
    rows = jnp.arange(number, dtype=jnp.int32)

    def row_turn(index, result):
        index = index.astype(jnp.int32)
        select = (rows == index).astype(jnp.float32)
        own_row = jnp.dot(select, factor, precision=HIGHEST)
        pivot = jnp.dot(own_row, select, precision=HIGHEST)
        value = (
            jnp.dot(select, right, precision=HIGHEST) - jnp.dot(own_row, result, precision=HIGHEST)
        ) / pivot
        return result + select[:, None] * value[None, :]

    return lax.fori_loop(0, number, row_turn, jnp.zeros_like(right))


def solve_upper_of(factor, right):
    number = factor.shape[0]
    rows = jnp.arange(number, dtype=jnp.int32)

    def row_turn(step, result):
        index = (number - 1 - step).astype(jnp.int32)
        select = (rows == index).astype(jnp.float32)
        own_row = jnp.dot(factor.T, select, precision=HIGHEST)
        pivot = jnp.dot(own_row, select, precision=HIGHEST)
        value = (
            jnp.dot(select, right, precision=HIGHEST) - jnp.dot(own_row, result, precision=HIGHEST)
        ) / pivot
        return result + select[:, None] * value[None, :]

    return lax.fori_loop(0, number, row_turn, jnp.zeros_like(right))


def fit_matrix(points):
    number = points.shape[1]
    vectors = OUTER * points[:, :, None] - INNER * points[:, None, :]
    kernel = green(vectors[0], vectors[1], vectors[2])
    normal = jnp.dot(kernel.T, kernel, precision=HIGHEST)
    ridge = REGULAR * jnp.trace(normal) / number
    normal = normal + ridge * jnp.eye(number, dtype=jnp.float32)
    factor = factor_lower(normal)
    middle = solve_lower(factor, kernel.T)
    return solve_upper_of(factor, middle)


def child_table(points, downward):
    half = jnp.array([-0.5, 0.5], dtype=jnp.float32)
    if downward:
        vectors = INNER * points[:, :, None] - PARENT_CHECK * points[:, None, :]
        sign = 1.0
    else:
        vectors = PARENT_CHECK * points[:, :, None] - INNER * points[:, None, :]
        sign = -1.0
    first = vectors[0][None, None, None] + sign * half[:, None, None, None, None]
    second = vectors[1][None, None, None] + sign * half[None, :, None, None, None]
    third = vectors[2][None, None, None] + sign * half[None, None, :, None, None]
    first, second, third = jnp.broadcast_arrays(first, second, third)
    return green(first, second, third)


def multiply_fit(checks, fit):
    return jnp.einsum("...k,jk->...j", checks, fit, precision=HIGHEST)


def apply_down(checks, fit):
    return jnp.einsum("...k,kj->...j", checks, fit, precision=HIGHEST)


def lift(child, up_table, fit):
    a, b, c, q = child.shape
    grouped = child.reshape(a // 2, 2, b // 2, 2, c // 2, 2, q)
    checks = jnp.einsum("axbyczk,xyzjk->abcj", grouped, up_table, precision=HIGHEST)
    return 2.0 * multiply_fit(checks, fit)


def descend(parent, down_table):
    a, b, c, q = parent.shape
    checks = jnp.einsum("abck,xyzjk->axbyczj", parent, down_table, precision=HIGHEST)
    return checks.reshape(2 * a, 2 * b, 2 * c, q)


def split_masked(array):
    slots = array.shape[-1] // 4
    positions = array[..., : 3 * slots].reshape(array.shape[:-1] + (3, slots))
    return (positions, array[..., 3 * slots :])


def upward_checks(positions, strengths, points):
    first = OUTER * points[0][:, None] - positions[..., 0, None, :]
    second = OUTER * points[1][:, None] - positions[..., 1, None, :]
    third = OUTER * points[2][:, None] - positions[..., 2, None, :]
    return jnp.sum(green(first, second, third) * strengths[..., None, :], axis=-1)


def local_values(positions, densities, points):
    first = positions[..., 0, :, None] - OUTER * points[0]
    second = positions[..., 1, :, None] - OUTER * points[1]
    third = positions[..., 2, :, None] - OUTER * points[2]
    return jnp.sum(green(first, second, third) * densities[..., None, :], axis=-1)


def pair_values(target_positions, source_positions, source_strengths, offset):
    first = target_positions[..., 0, :, None] - source_positions[..., 0, None, :] - offset[0]
    second = target_positions[..., 1, :, None] - source_positions[..., 1, None, :] - offset[1]
    third = target_positions[..., 2, :, None] - source_positions[..., 2, None, :] - offset[2]
    inverse = INV_FOUR_PI / jnp.sqrt(
        first * first + second * second + third * third + SOFTEN_SQUARED
    )
    return jnp.sum(inverse * source_strengths[..., None, :], axis=-1)


def list_kernels(offsets, points):
    first = INNER * (points[0][:, None] - points[0][None, :]) - offsets[:, 0, None, None]
    second = INNER * (points[1][:, None] - points[1][None, :]) - offsets[:, 1, None, None]
    third = INNER * (points[2][:, None] - points[2][None, :]) - offsets[:, 2, None, None]
    return green(first, second, third)


def far_kernels(delta, points):
    base = INNER * (points[:, :, None] - points[:, None, :])
    first = delta[:, 0, None, None] + base[0]
    second = delta[:, 1, None, None] + base[1]
    third = delta[:, 2, None, None] + base[2]
    spread = jnp.max(jnp.abs(delta), axis=1)
    return jnp.where((spread >= 2.0)[:, None, None], green(first, second, third), 0.0)


def allowed(shift, parity):
    return ((shift >= -2 - parity) & (shift <= 3 - parity)).astype(jnp.float32)


def widen(padded):
    return jnp.pad(padded, ((1, 1), (1, 1), (1, 1), (0, 0)))


def list_checks(padded, points):
    size_x = padded.shape[0] - 6
    size_y = padded.shape[1] - 6
    size_z = padded.shape[2] - 6
    parity_x = jnp.arange(size_x, dtype=jnp.int32) % 2
    parity_y = jnp.arange(size_y, dtype=jnp.int32) % 2
    parity_z = jnp.arange(size_z, dtype=jnp.int32) % 2
    depths = jnp.arange(7, dtype=jnp.int32) - 3
    valid_z = allowed(depths[:, None], parity_z[None, :])

    def x_turn(total, position):
        shift_x = position - 3
        slab = lax.dynamic_slice_in_dim(padded, position, size_x, 0)
        valid_x = allowed(shift_x, parity_x)
        for row in range(7):
            shift_y = row - 3
            valid_y = allowed(jnp.int32(shift_y), parity_y)
            pieces = jnp.stack(
                [slab[:, row : row + size_y, depth : depth + size_z, :] for depth in range(7)]
            )
            weights = (
                valid_x[None, :, None, None]
                * valid_y[None, None, :, None]
                * valid_z[:, None, None, :]
            )
            offsets = jnp.stack(
                [jnp.full((7,), shift_x), jnp.full((7,), shift_y, dtype=jnp.int32), depths], axis=1
            )
            offsets = offsets.astype(jnp.float32)
            spread = jnp.max(jnp.abs(offsets), axis=1)
            kernels = jnp.where((spread >= 2.0)[:, None, None], list_kernels(offsets, points), 0.0)
            total = total + jnp.einsum(
                "oxyzk,ojk->xyzj", pieces * weights[..., None], kernels, precision=HIGHEST
            )
        return (total, None)

    start_value = jnp.zeros((size_x, size_y, size_z, padded.shape[3]), jnp.float32)
    total, _ = lax.scan(x_turn, start_value, jnp.arange(7, dtype=jnp.int32))
    return total


def per_device(particles, counts):
    points = sphere(Q)
    fit = fit_matrix(points)
    up_table = child_table(points, False)
    down_table = child_table(points, True)
    side = particles.shape[0]
    depth = particles.shape[2] // side
    slots = particles.shape[3] // 4
    present = jnp.arange(slots, dtype=jnp.int32) < counts[..., None]
    masked = jnp.concatenate(
        [particles[..., : 3 * slots], jnp.where(present, particles[..., 3 * slots :], 0.0)], axis=3
    )
    positions, strengths = split_masked(masked)
    leaf_multipoles = multiply_fit(upward_checks(positions, strengths, points), fit)
    padded_near = extended(masked, (("gx", 0), ("gy", 1), ("gz", 2)), 1)
    padded_leaf = extended(leaf_multipoles, (("gx", 0), ("gy", 1), ("gz", 2)), 2)
    levels = side.bit_length() - 1
    multipoles = [leaf_multipoles]
    padded_levels = [padded_leaf]
    for level in range(1, levels):
        lifted = lift(multipoles[-1], up_table, fit)
        multipoles.append(lifted)
        padded_levels.append(extended(lifted, (("gx", 0), ("gy", 1), ("gz", 2)), 2))
    top_rows = lift(multipoles[-1], up_table, fit).reshape(depth, Q)
    grid_y = lax.axis_size("gy")
    grid_z = lax.axis_size("gz")
    devices = lax.axis_size("gx") * grid_y * grid_z
    layers = jnp.arange(depth, dtype=jnp.int32)
    own = jnp.stack(
        [
            jnp.broadcast_to(lax.axis_index("gx"), (depth,)),
            jnp.broadcast_to(lax.axis_index("gy"), (depth,)),
            lax.axis_index("gz") * depth + layers,
        ],
        axis=1,
    ).astype(jnp.float32)

    def box_coordinates(flat):
        device = flat // depth
        within = flat % depth
        return jnp.stack(
            [
                device // (grid_y * grid_z),
                device // grid_z % grid_y,
                device % grid_z * depth + within,
            ],
            axis=1,
        ).astype(jnp.float32)

    gathered = lax.all_gather(top_rows, ("gx", "gy", "gz"), axis=0, tiled=True)

    def block_term(total, number):
        rows = lax.dynamic_slice_in_dim(gathered, number * far_block, far_block, 0)
        flat = number * far_block + jnp.arange(far_block, dtype=jnp.int32)
        deltas = own[:, None, :] - box_coordinates(flat)[None, :, :]
        kernels = far_kernels(deltas.reshape(-1, 3), points).reshape(depth, far_block, Q, Q)
        return (total + jnp.einsum("dnjk,nk->dj", kernels, rows, precision=HIGHEST), None)

    far_check, _ = lax.scan(
        block_term,
        jnp.zeros((depth, Q), jnp.float32),
        jnp.arange(devices * depth // far_block, dtype=jnp.int32),
    )
    local = apply_down(far_check, fit).reshape(1, 1, depth, Q)
    for level in range(levels - 1, -1, -1):
        local = apply_down(
            list_checks(widen(padded_levels[level]), points) + descend(local, down_table), fit
        )
    far_part = local_values(positions, local, points)

    def near_turn(number, total):
        number = number.astype(jnp.int32)
        shift_x = number // 9
        shift_y = number // 3 % 3
        shift_z = number % 3
        block = lax.dynamic_slice(
            padded_near,
            (shift_x, shift_y, shift_z, jnp.int32(0)),
            (side, side, side * depth, 4 * slots),
        )
        source_positions, source_strengths = split_masked(block)
        offset = jnp.stack([shift_x, shift_y, shift_z]).astype(jnp.float32) - 1.0
        return total + pair_values(positions, source_positions, source_strengths, offset)

    near_part = lax.fori_loop(0, 27, near_turn, jnp.zeros_like(far_part))
    values = far_part + near_part
    return (
        values.reshape(side, side, side * depth * slots),
        near_part.reshape(side, side, side * depth * slots),
    )


def solution(mesh):
    placed = (P("gx", "gy", "gz", None), P("gx", "gy", "gz"))
    return jax.shard_map(
        per_device,
        mesh=mesh,
        in_specs=placed,
        out_specs=(P("gx", "gy", "gz"), P("gx", "gy", "gz")),
        check_vma=False,
    )
```

profile of v0, /device:TPU:0, one launch (start us, length us, event | category | flops | bytes accessed | tf_op | source)
XLA Modules:
  0.0 1426.6 jit_solution(13864986887942609)
XLA Ops:
  5.1 123.6 %while.112 = (s32[]{:T(128)}, f32[64,64]{1,0:T(8,128)S(1)}, f32[64,64]{1,0:T(8,128)S(1)}, s32[]{:T(128)}, s32[]{:T(128)}) while((s32[]{:T(128)}, f32[64,64]{1,0:T(8,128)S(1)}, f32[64,64]{1,0:T(8,128)S(1)}, s32[]{:T(128)}, s32[]{:T(128)}) %tuple.714), condition=%wide.region_3.4_spmd.clone.clone, body=%wide.region_2.3_spmd.clone.clone.sunk | while | flops 168642 | bytes 84589 | solution.py:65
  128.7 110.7 %while.109 = (s32[]{:T(128)}, f32[64,64]{1,0:T(8,128)S(1)}, f32[64,64]{1,0:T(8,128)S(1)}, f32[64,64]{1,0:T(8,128)S(1)}, s32[]{:T(128)}, /*index=5*/s32[]{:T(128)}) while((s32[]{:T(128)}, f32[64,64]{1,0:T(8,128)S(1)}, f32[64,64]{1,0:T(8,128)S(1)}, f32[64,64]{1,0:T(8,128)S(1)}, s32[]{:T(128)}, /*index=5*/s32[]{:T(128)}) %tuple.717), condition=%wide.region_5.6_spmd.clone, body=%wide.region_4.5_spmd.clone.sunk | while | flops 164418 | bytes 84068 | solution.py:82
  239.5 112.4 %while.110 = (s32[]{:T(128)}, f32[64,64]{1,0:T(8,128)S(1)}, f32[64,64]{1,0:T(8,128)S(1)}, f32[64,64]{1,0:T(8,128)S(1)}, s32[]{:T(128)}, /*index=5*/s32[]{:T(128)}, s32[]{:T(128)}) while((s32[]{:T(128)}, f32[64,64]{1,0:T(8,128)S(1)}, f32[64,64]{1,0:T(8,128)S(1)}, f32[64,64]{1,0:T(8,128)S(1)}, s32[]{:T(128)}, /*index=5*/s32[]{:T(128)}, ...), condition=%wide.region_7.8_spmd.clone, body=%wide.region_6.7_spmd.clone.sunk | while | flops 164419 | bytes 84088 | solution.py:99
  383.3 40.5 %all-reduce.3 = f32[2048]{0:T(1024)S(1)} all-reduce(f32[2048]{0:T(1024)S(1)} %dynamic-update-slice), channel_id=2, replica_groups=mesh['gx'=4,'gy'=4,'gz'=2] {'gx','gy','gz'}, use_global_device_ids=true, to_apply=%add.3 | all-reduce | flops 2048 | bytes 16384
  454.5 64.1 %while.115 = (s32[]{:T(128)}, f32[2,2,2,64]{3,2,0,1:T(2,128)S(1)}, s32[7]{0:T(128)S(1)}, f32[8,8,8,64]{3,2,1,0:T(8,128)S(1)}, s32[2]{0:T(128)S(1)}, /*index=5*/s...) while((s32[]{:T(128)}, f32[2,2,2,64]{3,2,0,1:T(2,128)S(1)}, ...), condition=%wide.region_34.35_spmd.clone.clone, body=%wide.region_26.34_spmd.clone.clone.sunk | while | flops 21332468 | bytes 1124439 | solution.py:241
  535.7 119.9 %while.114 = (s32[]{:T(128)}, f32[4,4,4,64]{3,2,0,1:T(4,128)}, s32[7]{0:T(128)}, f32[10,10,10,64]{3,2,1,0:T(8,128)S(1)}, s32[4]{0:T(128)}, /*index=5*/s32[4]{0:T...) while((s32[]{:T(128)}, f32[4,4,4,64]{3,2,0,1:T(4,128)}, ...), condition=%wide.region_25.26_spmd.clone.clone, body=%wide.region_17.25_spmd.clone.clone.sunk | while | flops 156412864 | bytes 7897751 | solution.py:241
  672.0 435.5 %while.111 = (s32[]{:T(128)}, f32[8,8,8,32]{3,2,1,0:T(8,128)}, f32[8,8,8,3,32]{4,2,1,0,3:T(8,128)S(1)}, f32[10,10,10,128]{3,2,1,0:T(8,128)S(1)}, s32[]{:T(128)},...) while((s32[]{:T(128)}, f32[8,8,8,32]{3,2,1,0:T(8,128)}, ...), condition=%wide.region_39.40_spmd.clone, body=%wide.region_37.39_spmd.clone.sunk | while | flops 7372849 | bytes 2949731 | solution.py:329
  674.2 13.3 multiply_reduce_fusion.4
  690.3 13.3 multiply_reduce_fusion.4
  706.4 13.3 multiply_reduce_fusion.4
  722.6 13.3 multiply_reduce_fusion.4
  738.7 13.3 multiply_reduce_fusion.4
  754.8 13.3 multiply_reduce_fusion.4
  771.0 13.3 multiply_reduce_fusion.4
  787.1 13.3 multiply_reduce_fusion.4
  803.2 13.3 multiply_reduce_fusion.4
  819.3 13.3 multiply_reduce_fusion.4
  835.5 13.3 multiply_reduce_fusion.4
  851.6 13.3 multiply_reduce_fusion.4
  867.7 13.3 multiply_reduce_fusion.4
  948.3 13.3 multiply_reduce_fusion.4
  1029.0 13.3 multiply_reduce_fusion.4
  1093.5 13.3 multiply_reduce_fusion.4
  1112.3 299.8 %while.113 = (s32[]{:T(128)}, f32[8,8,8,64]{3,2,0,1:T(8,128)}, s32[7]{0:T(128)S(1)}, f32[14,14,14,64]{3,2,1,0:T(8,128)S(1)}, s32[8]{0:T(128)S(1)}, /*index=5*/s3...) while((s32[]{:T(128)}, f32[8,8,8,64]{3,2,0,1:T(8,128)}, ...), condition=%wide.region_16.17_spmd.clone.clone, body=%wide.region_8.16_spmd.clone.clone.sunk | while | flops 1237054464 | bytes 67977432 | solution.py:241
  (4188 shorter events, 1045.6 us)
Async XLA Ops:
  364.9 61.9 %collective-permute-start.12 = (f32[2,2,2,64]{3,2,1,0:T(2,128)S(1)}, f32[2,2,2,64]{3,2,1,0:T(2,128)S(1)}, u32[]{:S(2)}, u32[]{:S(2)}) collective-permute-start(f32[2,2,2,64]{3,2,1,0:T(2,128)S(1)} %convolution_multiply_fusion.2), channel_id=1, source_target_pairs={{0,8},{8,16},{16,24},{1,9},{9,17},{17,25},{2,10},{10,18},{18,26},{... | collective-permute-start | bytes 6152 | tf_op jit(solution)/shard_map/ppermute | solution.py:29
  369.7 61.3 %collective-permute-start.13 = (f32[2,2,2,64]{3,2,1,0:T(2,128)S(1)}, f32[2,2,2,64]{3,2,1,0:T(2,128)S(1)}, u32[]{:S(2)}, u32[]{:S(2)}) collective-permute-start(f32[2,2,2,64]{3,2,1,0:T(2,128)S(1)} %convolution_multiply_fusion.2), channel_id=1, source_target_pairs={{8,0},{16,8},{24,16},{9,1},{17,9},{25,17},{10,2},{18,10},{26,18},{... | collective-permute-start | bytes 6152 | tf_op jit(solution)/shard_map/ppermute | solution.py:31
  371.1 149.1 %collective-permute-start.18 = (f32[1,8,8,128]{3,2,1,0:T(8,128)S(1)}, f32[1,8,8,128]{3,2,1,0:T(8,128)S(1)}, u32[]{:S(2)}, u32[]{:S(2)}) collective-permute-start(f32[1,8,8,128]{3,2,1,0:T(8,128)S(1)} %get-tuple-element.2511), channel_id=1, source_target_pairs={{0,8},{8,16},{16,24},{1,9},{9,17},{17,25},{2,10},{10,18},{18,26},{... | collective-permute-start | bytes 98312 | tf_op jit(solution)/shard_map/ppermute | solution.py:29
  375.7 145.9 %collective-permute-start.19 = (f32[1,8,8,128]{3,2,1,0:T(8,128)S(1)}, f32[1,8,8,128]{3,2,1,0:T(8,128)S(1)}, u32[]{:S(2)}, u32[]{:S(2)}) collective-permute-start(f32[1,8,8,128]{3,2,1,0:T(8,128)S(1)} %get-tuple-element.2512), channel_id=1, source_target_pairs={{8,0},{16,8},{24,16},{9,1},{17,9},{25,17},{10,2},{18,10},{26,18},{... | collective-permute-start | bytes 98312 | tf_op jit(solution)/shard_map/ppermute | solution.py:31
  377.0 149.3 %collective-permute-start = (f32[2,8,8,64]{3,2,1,0:T(8,128)S(1)}, f32[2,8,8,64]{3,2,1,0:T(8,128)S(1)}, u32[]{:S(2)}, u32[]{:S(2)}) collective-permute-start(f32[2,8,8,64]{3,2,1,0:T(8,128)S(1)} %get-tuple-element.2515), channel_id=1, source_target_pairs={{0,8},{8,16},{16,24},{1,9},{9,17},{17,25},{2,10},{10,18},{18,26},{... | collective-permute-start | bytes 98312 | tf_op jit(solution)/shard_map/ppermute | solution.py:29
  426.8 5.6 collective-permute-start.6
  431.0 5.6 collective-permute-start.7
  432.4 5.6 collective-permute-start.14
  436.7 5.9 collective-permute-start.15
  438.0 6.1 collective-permute-start.8
  442.6 5.8 collective-permute-start.9
  444.1 5.6 collective-permute-start.16
  448.4 3.1 collective-permute-start.17
  449.8 77.8 %collective-permute-start.1 = (f32[2,8,8,64]{3,2,1,0:T(8,128)S(1)}, f32[2,8,8,64]{3,2,1,0:T(8,128)S(1)}, u32[]{:S(2)}, u32[]{:S(2)}) collective-permute-start(f32[2,8,8,64]{3,2,1,0:T(8,128)S(1)} %get-tuple-element.2516), channel_id=1, source_target_pairs={{8,0},{16,8},{24,16},{9,1},{17,9},{25,17},{10,2},{18,10},{26,18},{... | collective-permute-start | bytes 98312 | tf_op jit(solution)/shard_map/ppermute | solution.py:31
  451.5 82.0 %collective-permute-start.10 = (f32[8,8,2,64]{3,2,1,0:T(2,128)S(1)}, f32[8,8,2,64]{3,2,1,0:T(2,128)S(1)}, u32[]{:S(2)}, u32[]{:S(2)}) collective-permute-start(f32[8,8,2,64]{3,2,1,0:T(2,128)S(1)} %get-tuple-element.2517), channel_id=1, source_target_pairs={{0,1},{2,3},{4,5},{6,7},{8,9},{10,11},{12,13},{14,15},{16,17},{18,... | collective-permute-start | bytes 98312 | tf_op jit(solution)/shard_map/ppermute | solution.py:29
  520.3 14.5 %collective-permute-start.11 = (f32[8,8,2,64]{3,2,1,0:T(2,128)S(1)}, f32[8,8,2,64]{3,2,1,0:T(2,128)S(1)}, u32[]{:S(2)}, u32[]{:S(2)}) collective-permute-start(f32[8,8,2,64]{3,2,1,0:T(2,128)S(1)} %get-tuple-element.2518), channel_id=1, source_target_pairs={{1,0},{3,2},{5,4},{7,6},{9,8},{11,10},{13,12},{15,14},{17,16},{19,... | collective-permute-start | bytes 98312 | tf_op jit(solution)/shard_map/ppermute | solution.py:31
  522.3 137.1 %collective-permute-start.20 = (f32[10,1,8,128]{3,2,1,0:T(8,128)}, f32[10,1,8,128]{3,2,1,0:T(8,128)}, u32[]{:S(2)}, u32[]{:S(2)}) collective-permute-start(f32[10,1,8,128]{3,2,1,0:T(8,128)} %get-tuple-element.2507), channel_id=1, source_target_pairs={{0,2},{2,4},{4,6},{1,3},{3,5},{5,7},{8,10},{10,12},{12,14},{9,11},... | collective-permute-start | bytes 122888 | tf_op jit(solution)/shard_map/ppermute | solution.py:29
  526.3 133.1 %collective-permute-start.21 = (f32[10,1,8,128]{3,2,1,0:T(8,128)}, f32[10,1,8,128]{3,2,1,0:T(8,128)}, u32[]{:S(2)}, u32[]{:S(2)}) collective-permute-start(f32[10,1,8,128]{3,2,1,0:T(8,128)} %get-tuple-element.2508), channel_id=1, source_target_pairs={{2,0},{4,2},{6,4},{3,1},{5,3},{7,5},{10,8},{12,10},{14,12},{11,9},... | collective-permute-start | bytes 122888 | tf_op jit(solution)/shard_map/ppermute | solution.py:31
  528.3 135.7 %collective-permute-start.2 = (f32[12,2,8,64]{3,2,1,0:T(8,128)}, f32[12,2,8,64]{3,2,1,0:T(8,128)}, u32[]{:S(2)}, u32[]{:S(2)}) collective-permute-start(f32[12,2,8,64]{3,2,1,0:T(8,128)} %get-tuple-element.2513), channel_id=1, source_target_pairs={{0,2},{2,4},{4,6},{1,3},{3,5},{5,7},{8,10},{10,12},{12,14},{9,11},... | collective-permute-start | bytes 147464 | tf_op jit(solution)/shard_map/ppermute | solution.py:29
  533.5 130.5 %collective-permute-start.3 = (f32[12,2,8,64]{3,2,1,0:T(8,128)}, f32[12,2,8,64]{3,2,1,0:T(8,128)}, u32[]{:S(2)}, u32[]{:S(2)}) collective-permute-start(f32[12,2,8,64]{3,2,1,0:T(8,128)} %get-tuple-element.2514), channel_id=1, source_target_pairs={{2,0},{4,2},{6,4},{3,1},{5,3},{7,5},{10,8},{12,10},{14,12},{11,9},... | collective-permute-start | bytes 147464 | tf_op jit(solution)/shard_map/ppermute | solution.py:31
  660.5 10.4 collective-permute-start.22
  662.7 8.2 collective-permute-start.23
  666.0 443.3 %collective-permute-start.4 = (f32[12,12,2,64]{3,2,1,0:T(2,128)}, f32[12,12,2,64]{3,2,1,0:T(2,128)}, u32[]{:S(2)}, u32[]{:S(2)}) collective-permute-start(f32[12,12,2,64]{3,2,1,0:T(2,128)} %get-tuple-element.2509), channel_id=1, source_target_pairs={{0,1},{2,3},{4,5},{6,7},{8,9},{10,11},{12,13},{14,15},{16,17},{18,... | collective-permute-start | bytes 221192 | tf_op jit(solution)/shard_map/ppermute | solution.py:29
  669.6 439.6 %collective-permute-start.5 = (f32[12,12,2,64]{3,2,1,0:T(2,128)}, f32[12,12,2,64]{3,2,1,0:T(2,128)}, u32[]{:S(2)}, u32[]{:S(2)}) collective-permute-start(f32[12,12,2,64]{3,2,1,0:T(2,128)} %get-tuple-element.2510), channel_id=1, source_target_pairs={{1,0},{3,2},{5,4},{7,6},{9,8},{11,10},{13,12},{15,14},{17,16},{19,... | collective-permute-start | bytes 221192 | tf_op jit(solution)/shard_map/ppermute | solution.py:31
  (426 other events, 2854.5 us)
where the time goes:
time: 1440 us; the launch traced here: 1430 us
  matrix products  499 us (35%)
  other arithmetic  457 us (32%)
  local copies, waits for them, and re-layouts  236 us (16%)
  loops' own time  126 us (9%)
  starting transfers between devices  61.1 us (4%)
  blocking collectives  40.5 us (3%)
    reduce_sum x27, other arithmetic, pair_values(): return jnp.sum(inverse * source_strengths[..., None, :], axis=-1)  358 us
    dot_general x147, matrix products, x_turn(): jnp.einsum('oxyzk,ojk->xyzj', pieces * weights[..., None], kernels, preci...  203 us
    while x1690, local copies, waits for them, and re-layouts  117 us
    dot_general x128, matrix products, row_turn(): jnp.dot(own_row, result, precision=HIGHEST)  100 us
    another operation x3, loops' own time, list_checks(): total, _ = lax.scan(x_turn, start_value, jnp.arange(7, dtype=jnp.int32))  78.2 us
    dot_general x64, matrix products, column_turn(): jnp.dot(factor, own_row, precision=HIGHEST)  56.6 us
    dot_general x64, matrix products, row_turn(): own_row = jnp.dot(select, factor, precision=HIGHEST)  48.1 us
    dot_general x64, matrix products, row_turn(): own_row = jnp.dot(factor.T, select, precision=HIGHEST)  47.8 us

commit v1 on v0

v1 whole, which is shorter than its diff:
```python
import math

import jax
import jax.numpy as jnp
import ml_dtypes
import numpy as np
from jax import lax
from jax.experimental import pallas as pl
from jax.experimental.pallas import tpu as pltpu
from jax.sharding import PartitionSpec as P

Q = 64
INV_FOUR_PI = 0.07957747154594767
INNER = 0.9
OUTER = 1.5
PARENT_CHECK = 3.0
SOFTEN_SQUARED = 0.0625
REGULAR = 0.01
HIGHEST = lax.Precision.HIGHEST
far_block = 32
AXES = ("gx", "gy", "gz")


def sphere(number):
    order = np.arange(number, dtype=np.float64)
    height = 1.0 - (2.0 * order + 1.0) / number
    radial = np.sqrt(1.0 - height * height)
    turning = order * (math.pi * (3.0 - math.sqrt(5.0)))
    return np.stack([radial * np.cos(turning), radial * np.sin(turning), height])


def green(vectors):
    return INV_FOUR_PI / np.sqrt(np.sum(vectors * vectors, axis=0))


def constant_tables():
    points = sphere(Q)
    kernel = green(OUTER * points[:, :, None] - INNER * points[:, None, :])
    normal = kernel.T @ kernel
    normal = normal + REGULAR * np.trace(normal) / Q * np.eye(Q)
    lower = np.linalg.cholesky(normal)
    fit = np.linalg.solve(lower, kernel.T) / np.diag(lower)[:, None]
    up = np.zeros((8 * Q, Q))
    down = np.zeros((Q, 8 * Q))
    for child in range(8):
        offset = np.array([child // 4, child // 2 % 2, child % 2]) - 0.5
        vectors = PARENT_CHECK * points[:, :, None] - INNER * points[:, None, :]
        upper = green(vectors - offset[:, None, None])
        up[child * Q : (child + 1) * Q] = (2.0 * fit @ upper).T
        vectors = INNER * points[:, :, None] - PARENT_CHECK * points[:, None, :]
        lower = green(vectors + offset[:, None, None])
        down[:, child * Q : (child + 1) * Q] = lower.T @ fit
    base = INNER * (points[:, :, None] - points[:, None, :])
    table = np.zeros((7, 7, 6, Q, 2, Q), np.float32)
    for ox in range(-3, 4):
        for oy in range(-3, 4):
            for sz in range(6):
                for cz in range(2):
                    offset = np.array([ox, oy, sz - 2 - cz], np.float64)
                    if np.max(np.abs(offset)) >= 2:
                        values = green(base - offset[:, None, None])
                        table[ox + 3, oy + 3, sz, :, cz, :] = values.T
    table = table.reshape(7, 7, 6 * Q, 2 * Q)
    high = table.astype(ml_dtypes.bfloat16)
    low = (table - high.astype(np.float32)).astype(ml_dtypes.bfloat16)
    spread = np.repeat((OUTER * points)[:, :, None], 128, axis=2).astype(np.float32)
    pair_fit = np.kron(np.eye(2), fit)
    single = np.float32
    return (
        points.astype(single),
        fit.astype(single),
        up.astype(single),
        down.astype(single),
        high,
        low,
        spread,
        pair_fit.astype(single),
    )


def dot(left, right):
    return jnp.dot(left, right, precision=HIGHEST, preferred_element_type=jnp.float32)


def upward_kernel(part, spread, fit_t, up, leaf, mid, coarse, top, turned):
    for block in range(4):
        turned[...] = part[pl.ds(128 * block, 128), :].T

        def slot_turn(p, total):
            first = spread[0] - turned[pl.ds(p, 1), :]
            second = spread[1] - turned[pl.ds(32 + p, 1), :]
            third = spread[2] - turned[pl.ds(64 + p, 1), :]
            strength = turned[pl.ds(96 + p, 1), :] * INV_FOUR_PI
            inverse = lax.rsqrt(first * first + second * second + third * third)
            return total + inverse * strength

        checks = lax.fori_loop(0, 32, slot_turn, jnp.zeros((Q, 128), jnp.float32))
        leaf[pl.ds(128 * block, 128), :] = dot(checks.T, fit_t[...])
    total = jnp.zeros((64, Q), jnp.float32)
    for child in range(8):
        total = total + dot(leaf[pl.ds(64 * child, 64), :], up[pl.ds(Q * child, Q), :])
    mid[...] = total
    total = jnp.zeros((8, Q), jnp.float32)
    for child in range(8):
        total = total + dot(mid[pl.ds(8 * child, 8), :], up[pl.ds(Q * child, Q), :])
    coarse[...] = total
    row = jnp.zeros((8, Q), jnp.float32)
    for child in range(8):
        own = jnp.broadcast_to(total[child : child + 1], (8, Q))
        row = row + dot(own, up[pl.ds(Q * child, Q), :])
    top[...] = row


def near_kernel(padded, out, rows):
    def pair_turn(pair, carry):
        start = 2 * pair

        def slab(ox, oy, oz):
            return jnp.concatenate(
                [
                    padded[start + ox, pl.ds(oy, 8), oz : oz + 8, :].reshape(64, 128),
                    padded[start + 1 + ox, pl.ds(oy, 8), oz : oz + 8, :].reshape(64, 128),
                ],
                axis=0,
            ).T

        own = slab(1, 1, 1)
        tx, ty, tz = own[0:32], own[32:64], own[64:96]
        square = tx * tx + ty * ty + tz * tz + SOFTEN_SQUARED

        def offset_turn(number, total):
            ox = number // 3
            oy = number % 3
            for oz in range(3):
                source = slab(ox, oy, oz)
                sx = source[0:32] + (ox - 1).astype(jnp.float32)
                sy = source[32:64] + (oy - 1).astype(jnp.float32)
                sz = source[64:96] + (oz - 1.0)
                rows[0:32] = -2.0 * sx
                rows[32:64] = -2.0 * sy
                rows[64:96] = -2.0 * sz
                rows[96:128] = sx * sx + sy * sy + sz * sz
                rows[128:160] = source[96:128] * INV_FOUR_PI

                def source_turn(p, total):
                    distance = (square + rows[pl.ds(96 + p, 1), :]) + (
                        tx * rows[pl.ds(p, 1), :]
                        + ty * rows[pl.ds(32 + p, 1), :]
                        + tz * rows[pl.ds(64 + p, 1), :]
                    )
                    return total + lax.rsqrt(distance) * rows[pl.ds(128 + p, 1), :]

                total = lax.fori_loop(0, 32, source_turn, total, unroll=8)
            return total

        total = lax.fori_loop(0, 9, offset_turn, jnp.zeros((32, 128), jnp.float32))
        out[pl.ds(pl.multiple_of(128 * pair, 128), 128), :] = total.T
        return carry

    lax.fori_loop(0, 4, pair_turn, 0)


def downward_kernel(
    windows, small, high, low, pair_fit, down, top_local, part, spread, out, total, turned, local
):
    total[...] = jnp.zeros_like(total)

    def source_turn(number, carry):
        sx = number // 6
        sy = number % 6
        pieces = []
        for cx in range(2):
            for cy in range(2):
                for cz in range(2):
                    pieces.append(windows[sx + 2 * cx, sy + 2 * cy, pl.ds(8 * cz, 8), :])
        pieces.append(small[sx, sy])
        left = jnp.concatenate(pieces, axis=0)
        left_high = left.astype(jnp.bfloat16)
        left_low = (left - left_high.astype(jnp.float32)).astype(jnp.bfloat16)
        both = jnp.concatenate([left_high, left_low], axis=0)
        places = [(sx + 1 - cx, sy + 1 - cy) for cx in range(2) for cy in range(2)]
        right_high = jnp.concatenate([high[a, b] for a, b in places], axis=1)
        right_low = jnp.concatenate([low[a, b] for a, b in places], axis=1)
        first = jnp.dot(both, right_high, preferred_element_type=jnp.float32)
        second = jnp.dot(left_high, right_low, preferred_element_type=jnp.float32)
        total[...] += first[:80] + first[80:] + second
        return carry

    lax.fori_loop(0, 36, source_turn, 0)
    fitted = jnp.concatenate(
        [dot(total[:, 128 * pair : 128 * pair + 128], pair_fit[...]) for pair in range(4)], axis=1
    )

    def regroup(rows):
        return jnp.concatenate([rows[:, Q * c : Q * c + Q] for c in range(8)], axis=0)

    coarse = fitted[72:80] + dot(top_local[...], down[...])
    coarse = regroup(coarse[0:1])
    mid = regroup(fitted[64:72] + dot(coarse, down[...]))
    leaf = fitted[0:64] + dot(mid, down[...])
    for block in range(4):
        turned[...] = part[pl.ds(128 * block, 128), :].T
        own = leaf[:, 128 * block : 128 * block + 128]
        own = jnp.concatenate([own[:, :Q], own[:, Q:]], axis=0)
        local[...] = own.T * INV_FOUR_PI
        tx, ty, tz = turned[0:32], turned[32:64], turned[64:96]

        def point_turn(k, value):
            first = tx - spread[0, pl.ds(k, 1), :]
            second = ty - spread[1, pl.ds(k, 1), :]
            third = tz - spread[2, pl.ds(k, 1), :]
            inverse = lax.rsqrt(first * first + second * second + third * third)
            return value + inverse * local[pl.ds(k, 1), :]

        value = lax.fori_loop(0, Q, point_turn, jnp.zeros((32, 128), jnp.float32), unroll=4)
        out[pl.ds(128 * block, 128), :] = value.T


def run(kernel, outs, scratch, cost, *args):
    return pl.pallas_call(
        kernel,
        out_shape=outs,
        scratch_shapes=[pltpu.VMEM(shape, jnp.float32) for shape in scratch],
        compiler_params=pltpu.CompilerParams(vmem_limit_bytes=40 << 20),
        cost_estimate=pl.CostEstimate(flops=cost, bytes_accessed=1 << 20, transcendentals=0),
    )(*args)


def single(*shape):
    return jax.ShapeDtypeStruct(shape, jnp.float32)


def nested(cells):
    split = cells.reshape((2,) * 9 + cells.shape[3:])
    return split.transpose(2, 5, 8, 1, 4, 7, 0, 3, 6, 9).reshape(512, -1)


def plain(rows):
    split = rows.reshape((2,) * 9 + rows.shape[1:])
    return split.transpose(6, 3, 0, 7, 4, 1, 8, 5, 2, 9).reshape(8, 8, 8, -1)


def plain_mid(rows):
    split = rows.reshape((2,) * 6 + rows.shape[1:])
    return split.transpose(3, 0, 4, 1, 5, 2, 6).reshape(4, 4, 4, -1)


def extended(arrays, width):
    for axis, dim in (("gz", 2), ("gy", 1), ("gx", 0)):
        count = lax.axis_size(axis)
        heads = [lax.slice_in_dim(a, 0, width, axis=dim) for a in arrays]
        tails = [lax.slice_in_dim(a, a.shape[dim] - width, a.shape[dim], axis=dim) for a in arrays]
        forward = [(i, i + 1) for i in range(count - 1)]
        backward = [(i + 1, i) for i in range(count - 1)]

        def pack(parts):
            return jnp.concatenate([x.reshape(-1, x.shape[-1]) for x in parts], axis=0)

        def unpack(rows, parts):
            result, start = [], 0
            for x in parts:
                length = x.size // x.shape[-1]
                result.append(rows[start : start + length].reshape(x.shape))
                start += length
            return result

        before = unpack(lax.ppermute(pack(tails), axis, forward), tails)
        after = unpack(lax.ppermute(pack(heads), axis, backward), heads)
        arrays = [
            jnp.concatenate([b, a, c], axis=dim) for b, a, c in zip(before, arrays, after)
        ]
    return arrays


def far_local(top_row, points, fit):
    grid_y = lax.axis_size("gy")
    grid_z = lax.axis_size("gz")
    devices = lax.axis_size("gx") * grid_y * grid_z
    gathered = lax.all_gather(top_row, AXES, axis=0, tiled=True)
    own = jnp.stack([lax.axis_index(axis) for axis in AXES]).astype(jnp.float32)
    base = INNER * (points[:, :, None] - points[:, None, :])

    def block_term(total, number):
        rows = lax.dynamic_slice_in_dim(gathered, number * far_block, far_block, 0)
        flat = number * far_block + jnp.arange(far_block, dtype=jnp.int32)
        boxes = jnp.stack(
            [flat // (grid_y * grid_z), flat // grid_z % grid_y, flat % grid_z], axis=1
        )
        delta = own[None, :] - boxes.astype(jnp.float32)
        spread = jnp.max(jnp.abs(delta), axis=1)
        first = delta[:, 0, None, None] + base[0]
        second = delta[:, 1, None, None] + base[1]
        third = delta[:, 2, None, None] + base[2]
        square = first * first + second * second + third * third
        kernels = jnp.where(
            (spread >= 2.0)[:, None, None], INV_FOUR_PI / jnp.sqrt(square), 0.0
        )
        return (total + jnp.sum(kernels * rows[:, None, :], axis=(0, 2)), None)

    blocks = devices // far_block
    check, _ = lax.scan(
        block_term, jnp.zeros((Q,), jnp.float32), jnp.arange(blocks, dtype=jnp.int32)
    )
    return jnp.dot(check[None, :], fit, precision=HIGHEST)


def per_device(particles, counts):
    points, fit, up, down, high, low, spread, pair_fit = constant_tables()
    slots = particles.shape[3] // 4
    present = jnp.arange(slots, dtype=jnp.int32) < counts[..., None]
    masked = jnp.concatenate(
        [particles[..., : 3 * slots], jnp.where(present, particles[..., 3 * slots :], 0.0)], axis=3
    )
    part = nested(masked)
    leaf, mid, coarse, top = run(
        upward_kernel,
        (single(512, Q), single(64, Q), single(8, Q), single(8, Q)),
        [(128, 128)],
        1 << 30,
        part,
        spread,
        np.ascontiguousarray(fit.T),
        up,
    )
    (padded_near,) = extended([masked], 1)
    near = run(near_kernel, single(512, 32), [(160, 128)], 30 << 30, padded_near)
    top_local = far_local(top[0:1], points, fit)
    leaf_cells, mid_cells, coarse_cells = extended(
        [plain(leaf), plain_mid(mid), coarse.reshape(2, 2, 2, Q)], 2
    )
    leaf_cells = leaf_cells.reshape(12, 12, 12 * Q)
    windows = jnp.stack(
        [
            leaf_cells[4 * gx : 4 * gx + 8, 4 * gy : 4 * gy + 8, Q * start : Q * start + 6 * Q]
            for cz in range(2)
            for gx in range(2)
            for gy in range(2)
            for start in (2 * cz, 4 + 2 * cz)
        ],
        axis=2,
    )
    mid_cells = mid_cells.reshape(8, 8, 8 * Q)
    small = jnp.stack(
        [
            mid_cells[2 * gx : 2 * gx + 6, 2 * gy : 2 * gy + 6, 2 * gz * Q : (2 * gz + 6) * Q]
            for gx in range(2)
            for gy in range(2)
            for gz in range(2)
        ]
        + [coarse_cells.reshape(6, 6, 6 * Q)]
        + [jnp.zeros((6, 6, 6 * Q), jnp.float32)] * 7,
        axis=2,
    )
    far = run(
        downward_kernel,
        single(512, 32),
        [(80, 512), (128, 128), (Q, 128)],
        8 << 30,
        windows,
        small,
        high,
        low,
        pair_fit,
        down,
        jnp.broadcast_to(top_local, (8, Q)),
        part,
        spread,
    )
    near = near.reshape(8, 8, 8 * slots)
    return (plain(far).reshape(8, 8, 8 * slots) + near, near)


def solution(mesh):
    placed = (P("gx", "gy", "gz", None), P("gx", "gy", "gz"))
    return jax.shard_map(
        per_device,
        mesh=mesh,
        in_specs=placed,
        out_specs=(P("gx", "gy", "gz"), P("gx", "gy", "gz")),
        check_vma=False,
    )
```

time: 1440 us -> 163 us (0.11)
  matrix products: 499 us -> 0.14 us
  other arithmetic: 457 us -> 5.02 us
  local copies, waits for them, and re-layouts: 236 us -> 26.3 us
  loops' own time: 126 us -> 0 us
  Pallas kernels: 0 us -> 53.7 us
  starting transfers between devices: 61.1 us -> 32.2 us
    dot_general x739 -> x1, matrix products: 499 us -> 0.14 us  [far_local(): return jnp.dot(check[None, :], fit, precision=HIGHEST)]
    reduce_sum x29 -> x1, other arithmetic: 380 us -> 0.68 us  [block_term(): return (total + jnp.sum(kernels * rows[:, None, :], axis=(0, 2)), None)]
    another operation x7 -> x0, loops' own time: 126 us -> none  [the longest x3 78.2 us: list_checks(): total, _ = lax.scan(x_turn, start_value, jnp.arange(7, dtype=jnp.int32))]
    while x1690 -> x0, local copies, waits for them, and re-layouts: 117 us -> none
    slice x107 -> x25, local copies, waits for them, and re-layouts: 75.3 us -> 0.27 us  [the longest x18 0.1 us: unpack(): result.append(rows[start:start + length].reshape(x.shape))]
    pallas_call x0 -> x3, Pallas kernels: none -> 53.7 us  [run(): pl.pallas_call(kernel, out_shape=outs, scratch_shapes=[pltpu.VMEM(shape,...]
    all_gather x0 -> x1, blocking collectives: none -> 43.1 us  [far_local(): gathered = lax.all_gather(top_row, AXES, axis=0, tiled=True)]
    unnamed x1 -> x0, blocking collectives: 40.5 us -> none
where the time goes in v1:
time: 163 us; the launch traced here: 162 us
  Pallas kernels  53.7 us (33%)
  blocking collectives  43.1 us (26%)
  starting transfers between devices  32.2 us (20%)
  local copies, waits for them, and re-layouts  26.3 us (16%)
  other arithmetic  5.02 us (3%)
    pallas_call x3, Pallas kernels, run(): pl.pallas_call(kernel, out_shape=outs, scratch_shapes=[pltpu.VMEM(shape,...  53.7 us
    all_gather x1, blocking collectives, far_local(): gathered = lax.all_gather(top_row, AXES, axis=0, tiled=True)  43.1 us
    ppermute x6, starting transfers between devices, extended(): before = unpack(lax.ppermute(pack(tails), axis, forward), tails)  24.5 us
    another operation x18, local copies, waits for them, and re-layouts, per_device(): jnp.stack([leaf_cells[4 * gx:4 * gx + 8, 4 * gy:4 * gy + 8, Q * start:Q *...  13.8 us
    ppermute x6, starting transfers between devices, extended(): after = unpack(lax.ppermute(pack(heads), axis, backward), heads)  7.73 us
    unnamed x29, local copies, waits for them, and re-layouts  7.37 us
  transfers between devices with their start and end apart: 12, of which 0 were waited for; matrix products, arithmetic and copies ran while one was open for 2% of the time, Pallas kernels for 21%

profile of v1, /device:TPU:0, one launch (start us, length us, event | category | flops | bytes accessed | tf_op | source)
XLA Modules:
  0.0 162.0 jit_solution(11328404271646791772)
XLA Ops:
  0.7 1.2 slice_select_fusion
  1.9 1.1 pad_maximum_fusion.5
  3.2 0.9 copy-done.2
  4.1 0.9 copy-done.4
  5.8 5.5 %shard_map.140 = (f32[512,64]{1,0:T(8,128)S(1)}, f32[64,64]{1,0:T(8,128)S(1)}, f32[8,64]{1,0:T(8,128)S(1)}, f32[8,64]{1,0:T(8,128)S(1)}) custom-call(f32[512,128]{1,0:T(8,128)S(1)} %bitcast.103, f32[3,64,128]{2,1,0:T(8,128)S(1)} %copy-done.4, f32[64,64]{1,0:T(8,128)S(1)} %copy-done.7, f32[512,64]{1,0:T(8,128)S(1)} %copy-done.2), custom_call_target="tpu_custom_call" | custom-call | flops 1073741824 | bytes 1048576 | tf_op jit(solution)/shard_map/pallas_call | solution.py:220
  11.6 1.3 collective-permute-start.1
  12.9 3.0 %collective-permute-start = (f32[168,64]{1,0:T(8,128)S(1)}, f32[168,64]{1,0:T(8,128)S(1)}, u32[]{:S(2)}, u32[]{:S(2)}) collective-permute-start(f32[168,64]{1,0:T(8,128)S(1)} %get-tuple-element.83), channel_id=1, source_target_pairs={{0,1},{2,3},{4,5},{6,7},{8,9},{10,11},{12,13},{14,15},{16,17},{18,... | collective-permute-start | bytes 129032 | tf_op jit(solution)/shard_map/ppermute | solution.py:267
  16.1 1.3 collective-permute-start.7
  17.4 3.0 %collective-permute-start.6 = (f32[64,128]{1,0:T(8,128)S(1)}, f32[64,128]{1,0:T(8,128)S(1)}, u32[]{:S(2)}, u32[]{:S(2)}) collective-permute-start(f32[64,128]{1,0:T(8,128)S(1)} %bitcast.154), channel_id=1, source_target_pairs={{0,1},{2,3},{4,5},{6,7},{8,9},{10,11},{12,13},{14,15},{16,17},{18,... | collective-permute-start | bytes 98312 | tf_op jit(solution)/shard_map/ppermute | solution.py:267
  20.5 43.1 %all-gather = f32[32,1,64]{2,1,0:T(1,128)S(1)} all-gather(f32[1,1,64]{2,1,0:T(1,128)S(1)} %slice_bitcast_fusion.22), channel_id=1, replica_groups=mesh['gx'=4,'gy'=4,'gz'=2] {'gx','gy','gz'}, dimensions={0}, use_global_device_ids=true | all-gather | bytes 8448 | tf_op jit(solution)/shard_map/all_gather | solution.py:279
  64.8 1.3 collective-permute-start.9
  66.1 4.5 %collective-permute-start.8 = (f32[80,128]{1,0:T(8,128)S(1)}, f32[80,128]{1,0:T(8,128)S(1)}, u32[]{:S(2)}, u32[]{:S(2)}) collective-permute-start(f32[80,128]{1,0:T(8,128)S(1)} %reshape.371), channel_id=1, source_target_pairs={{0,2},{2,4},{4,6},{1,3},{3,5},{5,7},{8,10},{10,12},{12,14},{9,11},... | collective-permute-start | bytes 122888 | tf_op jit(solution)/shard_map/ppermute | solution.py:267
  71.3 1.3 collective-permute-start.3
  72.6 4.6 %collective-permute-start.2 = (f32[280,64]{1,0:T(8,128)S(1)}, f32[280,64]{1,0:T(8,128)S(1)}, u32[]{:S(2)}, u32[]{:S(2)}) collective-permute-start(f32[280,64]{1,0:T(8,128)S(1)} %get-tuple-element.81), channel_id=1, source_target_pairs={{0,2},{2,4},{4,6},{1,3},{3,5},{5,7},{8,10},{10,12},{12,14},{9,11},... | collective-permute-start | bytes 215048 | tf_op jit(solution)/shard_map/ppermute | solution.py:267
  77.4 1.3 collective-permute-start.11
  78.7 4.5 %collective-permute-start.10 = (f32[100,128]{1,0:T(8,128)S(1)}, f32[100,128]{1,0:T(8,128)S(1)}, u32[]{:S(2)}, u32[]{:S(2)}) collective-permute-start(f32[100,128]{1,0:T(8,128)S(1)} %reshape.375), channel_id=1, source_target_pairs={{0,8},{8,16},{16,24},{1,9},{9,17},{17,25},{2,10},{10,18},{18,26},{... | collective-permute-start | bytes 153608 | tf_op jit(solution)/shard_map/ppermute | solution.py:267
  84.2 1.3 collective-permute-start.5
  85.5 4.7 %collective-permute-start.4 = (f32[488,64]{1,0:T(8,128)S(1)}, f32[488,64]{1,0:T(8,128)S(1)}, u32[]{:S(2)}, u32[]{:S(2)}) collective-permute-start(f32[488,64]{1,0:T(8,128)S(1)} %get-tuple-element.78), channel_id=1, source_target_pairs={{0,8},{8,16},{16,24},{1,9},{9,17},{17,25},{2,10},{10,18},{18,26},{... | collective-permute-start | bytes 374792 | tf_op jit(solution)/shard_map/ppermute | solution.py:267
  90.5 33.6 %shard_map.142 = f32[512,32]{1,0:T(8,128)S(1)} custom-call(f32[10,10,10,128]{3,2,1,0:T(8,128)S(1)} %pad_maximum_fusion.padded), custom_call_target="tpu_custom_call" | custom-call | flops 32212254720 | bytes 1048576 | tf_op jit(solution)/shard_map/pallas_call | solution.py:220
  135.2 1.2 stack.133.small
  136.5 5.1 %stack.122.windows = f32[8,8,16,384]{3,2,1,0:T(8,128)S(1)} concatenate(f32[8,8,1,384]{3,2,1,0:T(1,128)S(1)} %copy.106, f32[8,8,1,384]{3,2,1,0:T(1,128)S(1)} %copy.107, f32[8,8,1,384]{3,2,1,0:T(1,128)S(1)} %copy.108, f32[8,8,1,384]{3,2,1,0:T(1,128)S(1)} %copy.109, f32[8,8,1,384]{3,2,1,0:T(1,128)S(1)} %copy.110, f32[8,8,1,384]{3,2,1,0:T(1,128)} %copy.111, f32[8,8,1,384]{3,2,1,0:T(1,128)} %copy.112, ...), dimensions={2} | concatenate | bytes 3145728 | tf_op jit(solution)/shard_map/stack | solution.py:332
  141.6 2.4 %copy-done = bf16[7,7,384,128]{3,2,1,0:T(8,128)(2,1)S(1)} copy-done((bf16[7,7,384,128]{3,2,1,0:T(8,128)(2,1)S(1)}, bf16[7,7,384,128]{3,2,1,0:T(8,128)(2,1)}, u32[]{:S(2)}) %copy-start) | copy-done | bytes 4816920
  144.0 2.4 %copy-done.1 = bf16[7,7,384,128]{3,2,1,0:T(8,128)(2,1)S(1)} copy-done((bf16[7,7,384,128]{3,2,1,0:T(8,128)(2,1)S(1)}, bf16[7,7,384,128]{3,2,1,0:T(8,128)(2,1)}, u32[]{:S(2)}) %copy-start.1) | copy-done | bytes 4816920
  146.3 14.5 %shard_map.141 = f32[512,32]{1,0:T(8,128)S(1)} custom-call(f32[8,8,16,384]{3,2,1,0:T(8,128)S(1)} %stack.122.windows, f32[6,6,16,384]{3,2,1,0:T(8,128)S(1)} %stack.133.small, bf16[7,7,384,128]{3,2,1,0:T(8,128)(2,1)S(1)} %copy-done, bf16[7,7,384,128]{3,2,1,0:T(8,128)(2,1)S(1)} %copy-done.1, f32[128,128]{1,0:T(8,128)S(1)} %copy-done.6, ...), custom_call_target="tpu_custom_call" | custom-call | flops 8589934592 | bytes 1048576 | tf_op jit(solution)/shard_map/pallas_call | solution.py:220
  (156 shorter events, 16.3 us)
Async XLA Ops:
  0.6 63.1 %copy-start.11 = (f32[64,64]{1,0:T(8,128)S(1)}, f32[64,64]{1,0:T(8,128)}, u32[]{:S(2)}) copy-start(f32[64,64]{1,0:T(8,128)} %constant.119.clone) | copy-start | bytes 49156
  0.6 63.1 %copy-start.12 = (f32[64,64]{1,0:T(8,128)S(1)}, f32[64,64]{1,0:T(8,128)}, u32[]{:S(2)}) copy-start(f32[64,64]{1,0:T(8,128)} %constant.118.clone) | copy-start | bytes 49156
  0.7 63.1 %copy-start.13 = (f32[64,64]{1,0:T(8,128)S(1)}, f32[64,64]{1,0:T(8,128)}, u32[]{:S(2)}) copy-start(f32[64,64]{1,0:T(8,128)} %constant.117.clone) | copy-start | bytes 49156
  0.7 63.8 %copy-start.10 = (f32[64,64]{1,0:T(8,128)S(1)}, f32[64,64]{1,0:T(8,128)}, u32[]{:S(2)}) copy-start(f32[64,64]{1,0:T(8,128)} %constant.120.clone) | copy-start | bytes 49156
  0.7 15.3 %copy-start.8 = (f32[8,8,8,128]{3,2,1,0:T(8,128)S(1)}, f32[8,8,8,128]{3,2,1,0:T(8,128)}, u32[]{:S(2)}) copy-start(f32[8,8,8,128]{3,2,1,0:T(8,128)} %param.13) | copy-start | bytes 786436
  3.2 1.0 copy-start.2
  11.6 59.1 %collective-permute-start.1 = (f32[168,64]{1,0:T(8,128)S(1)}, f32[168,64]{1,0:T(8,128)S(1)}, u32[]{:S(2)}, u32[]{:S(2)}) collective-permute-start(f32[168,64]{1,0:T(8,128)S(1)} %get-tuple-element.84), channel_id=1, source_target_pairs={{1,0},{3,2},{5,4},{7,6},{9,8},{11,10},{13,12},{15,14},{17,16},{19,... | collective-permute-start | bytes 129032 | tf_op jit(solution)/shard_map/ppermute | solution.py:268
  12.9 57.8 %collective-permute-start = (f32[168,64]{1,0:T(8,128)S(1)}, f32[168,64]{1,0:T(8,128)S(1)}, u32[]{:S(2)}, u32[]{:S(2)}) collective-permute-start(f32[168,64]{1,0:T(8,128)S(1)} %get-tuple-element.83), channel_id=1, source_target_pairs={{0,1},{2,3},{4,5},{6,7},{8,9},{10,11},{12,13},{14,15},{16,17},{18,... | collective-permute-start | bytes 129032 | tf_op jit(solution)/shard_map/ppermute | solution.py:267
  16.1 48.5 %collective-permute-start.7 = (f32[64,128]{1,0:T(8,128)S(1)}, f32[64,128]{1,0:T(8,128)S(1)}, u32[]{:S(2)}, u32[]{:S(2)}) collective-permute-start(f32[64,128]{1,0:T(8,128)S(1)} %bitcast.155), channel_id=1, source_target_pairs={{1,0},{3,2},{5,4},{7,6},{9,8},{11,10},{13,12},{15,14},{17,16},{19,... | collective-permute-start | bytes 98312 | tf_op jit(solution)/shard_map/ppermute | solution.py:268
  17.4 47.2 %collective-permute-start.6 = (f32[64,128]{1,0:T(8,128)S(1)}, f32[64,128]{1,0:T(8,128)S(1)}, u32[]{:S(2)}, u32[]{:S(2)}) collective-permute-start(f32[64,128]{1,0:T(8,128)S(1)} %bitcast.154), channel_id=1, source_target_pairs={{0,1},{2,3},{4,5},{6,7},{8,9},{10,11},{12,13},{14,15},{16,17},{18,... | collective-permute-start | bytes 98312 | tf_op jit(solution)/shard_map/ppermute | solution.py:267
  64.8 12.4 %collective-permute-start.9 = (f32[80,128]{1,0:T(8,128)S(1)}, f32[80,128]{1,0:T(8,128)S(1)}, u32[]{:S(2)}, u32[]{:S(2)}) collective-permute-start(f32[80,128]{1,0:T(8,128)S(1)} %reshape.373), channel_id=1, source_target_pairs={{2,0},{4,2},{6,4},{3,1},{5,3},{7,5},{10,8},{12,10},{14,12},{11,9},... | collective-permute-start | bytes 122888 | tf_op jit(solution)/shard_map/ppermute | solution.py:268
  66.1 11.1 %collective-permute-start.8 = (f32[80,128]{1,0:T(8,128)S(1)}, f32[80,128]{1,0:T(8,128)S(1)}, u32[]{:S(2)}, u32[]{:S(2)}) collective-permute-start(f32[80,128]{1,0:T(8,128)S(1)} %reshape.371), channel_id=1, source_target_pairs={{0,2},{2,4},{4,6},{1,3},{3,5},{5,7},{8,10},{10,12},{12,14},{9,11},... | collective-permute-start | bytes 122888 | tf_op jit(solution)/shard_map/ppermute | solution.py:267
  71.3 11.9 %collective-permute-start.3 = (f32[280,64]{1,0:T(8,128)S(1)}, f32[280,64]{1,0:T(8,128)S(1)}, u32[]{:S(2)}, u32[]{:S(2)}) collective-permute-start(f32[280,64]{1,0:T(8,128)S(1)} %get-tuple-element.82), channel_id=1, source_target_pairs={{2,0},{4,2},{6,4},{3,1},{5,3},{7,5},{10,8},{12,10},{14,12},{11,9},... | collective-permute-start | bytes 215048 | tf_op jit(solution)/shard_map/ppermute | solution.py:268
  72.6 10.6 %collective-permute-start.2 = (f32[280,64]{1,0:T(8,128)S(1)}, f32[280,64]{1,0:T(8,128)S(1)}, u32[]{:S(2)}, u32[]{:S(2)}) collective-permute-start(f32[280,64]{1,0:T(8,128)S(1)} %get-tuple-element.81), channel_id=1, source_target_pairs={{0,2},{2,4},{4,6},{1,3},{3,5},{5,7},{8,10},{10,12},{12,14},{9,11},... | collective-permute-start | bytes 215048 | tf_op jit(solution)/shard_map/ppermute | solution.py:267
  77.4 12.9 %collective-permute-start.11 = (f32[100,128]{1,0:T(8,128)S(1)}, f32[100,128]{1,0:T(8,128)S(1)}, u32[]{:S(2)}, u32[]{:S(2)}) collective-permute-start(f32[100,128]{1,0:T(8,128)S(1)} %reshape.377), channel_id=1, source_target_pairs={{8,0},{16,8},{24,16},{9,1},{17,9},{25,17},{10,2},{18,10},{26,18},{... | collective-permute-start | bytes 153608 | tf_op jit(solution)/shard_map/ppermute | solution.py:268
  78.7 11.6 %collective-permute-start.10 = (f32[100,128]{1,0:T(8,128)S(1)}, f32[100,128]{1,0:T(8,128)S(1)}, u32[]{:S(2)}, u32[]{:S(2)}) collective-permute-start(f32[100,128]{1,0:T(8,128)S(1)} %reshape.375), channel_id=1, source_target_pairs={{0,8},{8,16},{16,24},{1,9},{9,17},{17,25},{2,10},{10,18},{18,26},{... | collective-permute-start | bytes 153608 | tf_op jit(solution)/shard_map/ppermute | solution.py:267
  84.2 40.7 %collective-permute-start.5 = (f32[488,64]{1,0:T(8,128)S(1)}, f32[488,64]{1,0:T(8,128)S(1)}, u32[]{:S(2)}, u32[]{:S(2)}) collective-permute-start(f32[488,64]{1,0:T(8,128)S(1)} %get-tuple-element.77), channel_id=1, source_target_pairs={{8,0},{16,8},{24,16},{9,1},{17,9},{25,17},{10,2},{18,10},{26,18},{... | collective-permute-start | bytes 374792 | tf_op jit(solution)/shard_map/ppermute | solution.py:268
  85.5 39.6 %collective-permute-start.4 = (f32[488,64]{1,0:T(8,128)S(1)}, f32[488,64]{1,0:T(8,128)S(1)}, u32[]{:S(2)}, u32[]{:S(2)}) collective-permute-start(f32[488,64]{1,0:T(8,128)S(1)} %get-tuple-element.78), channel_id=1, source_target_pairs={{0,8},{8,16},{16,24},{1,9},{9,17},{17,25},{2,10},{10,18},{18,26},{... | collective-permute-start | bytes 374792 | tf_op jit(solution)/shard_map/ppermute | solution.py:267
  130.4 11.2 %copy-start.3 = (f32[64,512]{1,0:T(8,128)S(1)}, f32[64,512]{1,0:T(8,128)}, u32[]{:S(2)}) copy-start(f32[64,512]{1,0:T(8,128)} %constant.124.clone.down) | copy-start | bytes 393220
  130.4 11.2 %copy-start.5 = (f32[3,64,128]{2,1,0:T(8,128)S(1)}, f32[3,64,128]{2,1,0:T(8,128)}, u32[]{:S(2)}) copy-start(f32[3,64,128]{2,1,0:T(8,128)} %constant.114.clone.spread) | copy-start | bytes 294916
  130.4 11.2 %copy-start.6 = (f32[128,128]{1,0:T(8,128)S(1)}, f32[128,128]{1,0:T(8,128)}, u32[]{:S(2)}) copy-start(f32[128,128]{1,0:T(8,128)} %constant.123.clone.pair_fit) | copy-start | bytes 196612
  141.6 2.4 %copy-start = (bf16[7,7,384,128]{3,2,1,0:T(8,128)(2,1)S(1)}, bf16[7,7,384,128]{3,2,1,0:T(8,128)(2,1)}, u32[]{:S(2)}) copy-start(bf16[7,7,384,128]{3,2,1,0:T(8,128)(2,1)} %constant.121.clone.high) | copy-start | bytes 14450692
  144.0 2.4 %copy-start.1 = (bf16[7,7,384,128]{3,2,1,0:T(8,128)(2,1)S(1)}, bf16[7,7,384,128]{3,2,1,0:T(8,128)(2,1)}, u32[]{:S(2)}) copy-start(bf16[7,7,384,128]{3,2,1,0:T(8,128)(2,1)} %constant.122.clone.low) | copy-start | bytes 14450692
  146.3 15.0 %copy-start.9 = (f32[8,8,256]{2,1,0:T(8,128)S(1)}, f32[8,8,256]{2,1,0:T(8,128)}, u32[]{:S(2)}) copy-start(f32[8,8,256]{2,1,0:T(8,128)} %reshape.379) | copy-start | bytes 196612
  (2 other events, 1.7 us)

commit v2 on v1

--- a/solution.py
+++ b/solution.py
@@ -1,3 +1,4 @@
+import functools
 import math
 
 import jax
@@ -111,53 +112,48 @@
     top[...] = row
 
 
-def near_kernel(padded, out, rows):
-    def pair_turn(pair, carry):
-        start = 2 * pair
-
-        def slab(ox, oy, oz):
-            return jnp.concatenate(
-                [
-                    padded[start + ox, pl.ds(oy, 8), oz : oz + 8, :].reshape(64, 128),
-                    padded[start + 1 + ox, pl.ds(oy, 8), oz : oz + 8, :].reshape(64, 128),
-                ],
-                axis=0,
-            ).T
-
-        own = slab(1, 1, 1)
-        tx, ty, tz = own[0:32], own[32:64], own[64:96]
-        square = tx * tx + ty * ty + tz * tz + SOFTEN_SQUARED
-
-        def offset_turn(number, total):
-            ox = number // 3
-            oy = number % 3
-            for oz in range(3):
-                source = slab(ox, oy, oz)
-                sx = source[0:32] + (ox - 1).astype(jnp.float32)
-                sy = source[32:64] + (oy - 1).astype(jnp.float32)
-                sz = source[64:96] + (oz - 1.0)
-                rows[0:32] = -2.0 * sx
-                rows[32:64] = -2.0 * sy
-                rows[64:96] = -2.0 * sz
-                rows[96:128] = sx * sx + sy * sy + sz * sz
-                rows[128:160] = source[96:128] * INV_FOUR_PI
-
-                def source_turn(p, total):
-                    distance = (square + rows[pl.ds(96 + p, 1), :]) + (
-                        tx * rows[pl.ds(p, 1), :]
-                        + ty * rows[pl.ds(32 + p, 1), :]
-                        + tz * rows[pl.ds(64 + p, 1), :]
-                    )
-                    return total + lax.rsqrt(distance) * rows[pl.ds(128 + p, 1), :]
-
-                total = lax.fori_loop(0, 32, source_turn, total, unroll=8)
-            return total
-
-        total = lax.fori_loop(0, 9, offset_turn, jnp.zeros((32, 128), jnp.float32))
-        out[pl.ds(pl.multiple_of(128 * pair, 128), 128), :] = total.T
-        return carry
-
-    lax.fori_loop(0, 4, pair_turn, 0)
+def near_kernel(start, padded, out, rows):
+
+    def slab(ox, oy, oz):
+        return jnp.concatenate(
+            [
+                padded[start + ox, pl.ds(oy, 8), oz : oz + 8, :].reshape(64, 128),
+                padded[start + 1 + ox, pl.ds(oy, 8), oz : oz + 8, :].reshape(64, 128),
+            ],
+            axis=0,
+        ).T
+
+    own = slab(1, 1, 1)
+    tx, ty, tz = own[0:32], own[32:64], own[64:96]
+    square = tx * tx + ty * ty + tz * tz + SOFTEN_SQUARED
+
+    def offset_turn(number, total):
+        ox = number // 3
+        oy = number % 3
+        for oz in range(3):
+            source = slab(ox, oy, oz)
+            sx = source[0:32] + (ox - 1).astype(jnp.float32)
+            sy = source[32:64] + (oy - 1).astype(jnp.float32)
+            sz = source[64:96] + (oz - 1.0)
+            rows[0:32] = -2.0 * sx
+            rows[32:64] = -2.0 * sy
+            rows[64:96] = -2.0 * sz
+            rows[96:128] = sx * sx + sy * sy + sz * sz
+            rows[128:160] = source[96:128] * INV_FOUR_PI
+
+            def source_turn(p, total):
+                distance = (square + rows[pl.ds(96 + p, 1), :]) + (
+                    tx * rows[pl.ds(p, 1), :]
+                    + ty * rows[pl.ds(32 + p, 1), :]
+                    + tz * rows[pl.ds(64 + p, 1), :]
+                )
+                return total + lax.rsqrt(distance) * rows[pl.ds(128 + p, 1), :]
+
+            total = lax.fori_loop(0, 32, source_turn, total, unroll=8)
+        return total
+
+    total = lax.fori_loop(0, 9, offset_turn, jnp.zeros((32, 128), jnp.float32))
+    out[...] = total.T
 
 
 def downward_kernel(
@@ -273,19 +269,27 @@
 
 
 def far_local(top_row, points, fit):
-    grid_y = lax.axis_size("gy")
-    grid_z = lax.axis_size("gz")
-    devices = lax.axis_size("gx") * grid_y * grid_z
-    gathered = lax.all_gather(top_row, AXES, axis=0, tiled=True)
+    gathered = top_row
+    index = jnp.zeros((1, 3), jnp.int32) + jnp.stack([lax.axis_index(axis) for axis in AXES])
+    for place, axis in ((2, "gz"), (1, "gy"), (0, "gx")):
+        count = lax.axis_size(axis)
+        step, length = 1, gathered.shape[0]
+        while step < count:
+            take = min(step, count - step) * length
+            ring = [(i, (i + step) % count) for i in range(count)]
+            arrived = lax.ppermute(gathered[:take], axis, ring)
+            from_index = index[:take, place] + (count - step)
+            from_index = jnp.where(from_index >= count, from_index - count, from_index)
+            moved = index[:take].at[:, place].set(from_index)
+            gathered = jnp.concatenate([gathered, arrived], axis=0)
+            index = jnp.concatenate([index, moved], axis=0)
+            step *= 2
     own = jnp.stack([lax.axis_index(axis) for axis in AXES]).astype(jnp.float32)
     base = INNER * (points[:, :, None] - points[:, None, :])
 
     def block_term(total, number):
         rows = lax.dynamic_slice_in_dim(gathered, number * far_block, far_block, 0)
-        flat = number * far_block + jnp.arange(far_block, dtype=jnp.int32)
-        boxes = jnp.stack(
-            [flat // (grid_y * grid_z), flat // grid_z % grid_y, flat % grid_z], axis=1
-        )
+        boxes = lax.dynamic_slice_in_dim(index, number * far_block, far_block, 0)
         delta = own[None, :] - boxes.astype(jnp.float32)
         spread = jnp.max(jnp.abs(delta), axis=1)
         first = delta[:, 0, None, None] + base[0]
@@ -297,7 +301,7 @@
         )
         return (total + jnp.sum(kernels * rows[:, None, :], axis=(0, 2)), None)
 
-    blocks = devices // far_block
+    blocks = gathered.shape[0] // far_block
     check, _ = lax.scan(
         block_term, jnp.zeros((Q,), jnp.float32), jnp.arange(blocks, dtype=jnp.int32)
     )
@@ -323,7 +327,19 @@
         up,
     )
     (padded_near,) = extended([masked], 1)
-    near = run(near_kernel, single(512, 32), [(160, 128)], 30 << 30, padded_near)
+    near = jnp.concatenate(
+        [
+            run(
+                functools.partial(near_kernel, start),
+                single(128, 32),
+                [(160, 128)],
+                8 << 30,
+                padded_near,
+            )
+            for start in (0, 2, 4, 6)
+        ],
+        axis=0,
+    )
     top_local = far_local(top[0:1], points, fit)
     leaf_cells, mid_cells, coarse_cells = extended(
         [plain(leaf), plain_mid(mid), coarse.reshape(2, 2, 2, Q)], 2

time: 163 us -> 146 us (0.90)
  blocking collectives: 43.1 us -> 0 us
  waiting for transfers between devices: 0.04 us -> 10.9 us
  starting transfers between devices: 32.2 us -> 40 us
  other arithmetic: 5.02 us -> 9.09 us
    all_gather x1 -> x0, blocking collectives: 43.1 us -> none  [far_local(): gathered = lax.all_gather(top_row, AXES, axis=0, tiled=True)]
    ppermute x0 -> x5, waiting for transfers between devices: none -> 10.9 us  [far_local(): arrived = lax.ppermute(gathered[:take], axis, ring)]
    ppermute x0 -> x5, starting transfers between devices: none -> 7.78 us  [far_local(): arrived = lax.ppermute(gathered[:take], axis, ring)]
    another operation x0 -> x6, other arithmetic: none -> 4.02 us
    pallas_call x3 -> x6, Pallas kernels: 53.7 us -> 53.8 us  [run(): pl.pallas_call(kernel, out_shape=outs, scratch_shapes=[pltpu.VMEM(shape,...]
  transfers between devices with their start and end apart: 12 -> 17, of which waited for: 0 -> 4; matrix products, arithmetic and copies ran while one was open for 2% -> 7% of each run, Pallas kernels for 21% -> 23%
where the time goes in v2:
time: 146 us; the launch traced here: 145 us
  Pallas kernels  53.8 us (37%)
  starting transfers between devices  40 us (27%)
  local copies, waits for them, and re-layouts  27.8 us (19%)
  waiting for transfers between devices  10.9 us (7%)
  other arithmetic  9.09 us (6%)
  between operations  2.95 us (2%)
    pallas_call x6, Pallas kernels, run(): pl.pallas_call(kernel, out_shape=outs, scratch_shapes=[pltpu.VMEM(shape,...  53.8 us
    ppermute x6, starting transfers between devices, extended(): before = unpack(lax.ppermute(pack(tails), axis, forward), tails)  24.5 us
    another operation x18, local copies, waits for them, and re-layouts, per_device(): jnp.stack([leaf_cells[4 * gx:4 * gx + 8, 4 * gy:4 * gy + 8, Q * start:Q *...  13.7 us
    ppermute x5, waiting for transfers between devices, far_local(): arrived = lax.ppermute(gathered[:take], axis, ring)  10.9 us
    ppermute x5, starting transfers between devices, far_local(): arrived = lax.ppermute(gathered[:take], axis, ring)  7.78 us
    ppermute x6, starting transfers between devices, extended(): after = unpack(lax.ppermute(pack(heads), axis, backward), heads)  7.73 us
    unnamed x29, local copies, waits for them, and re-layouts  7.37 us
    another operation x6, other arithmetic  4.02 us
  transfers between devices with their start and end apart: 17, of which 4 were waited for; matrix products, arithmetic and copies ran while one was open for 7% of the time, Pallas kernels for 23%

profile of v2, /device:TPU:0, one launch (start us, length us, event | category | flops | bytes accessed | tf_op | source)
XLA Modules:
  0.0 144.6 jit_solution(12439814641963097101)
XLA Ops:
  5.8 5.5 %shard_map.140 = (f32[512,64]{1,0:T(8,128)S(1)}, f32[64,64]{1,0:T(8,128)S(1)}, f32[8,64]{1,0:T(8,128)S(1)}, f32[8,64]{1,0:T(8,128)S(1)}) custom-call(f32[512,128]{1,0:T(8,128)S(1)} %bitcast.104, f32[3,64,128]{2,1,0:T(8,128)S(1)} %copy-done.4, f32[64,64]{1,0:T(8,128)S(1)} %copy-done.7, f32[512,64]{1,0:T(8,128)S(1)} %copy-done.2), custom_call_target="tpu_custom_call" | custom-call | flops 1073741824 | bytes 1048576 | tf_op jit(solution)/shard_map/pallas_call | solution.py:216
  11.6 1.3 collective-permute-start.1
  12.9 3.0 %collective-permute-start = (f32[168,64]{1,0:T(8,128)S(1)}, f32[168,64]{1,0:T(8,128)S(1)}, u32[]{:S(2)}, u32[]{:S(2)}) collective-permute-start(f32[168,64]{1,0:T(8,128)S(1)} %get-tuple-element.148), channel_id=1, source_target_pairs={{0,1},{2,3},{4,5},{6,7},{8,9},{10,11},{12,13},{14,15},{16,17},{18,... | collective-permute-start | bytes 129032 | tf_op jit(solution)/shard_map/ppermute | solution.py:263
  16.2 1.3 collective-permute-start.12
  17.5 3.0 %collective-permute-start.11 = (f32[64,128]{1,0:T(8,128)S(1)}, f32[64,128]{1,0:T(8,128)S(1)}, u32[]{:S(2)}, u32[]{:S(2)}) collective-permute-start(f32[64,128]{1,0:T(8,128)S(1)} %bitcast.155), channel_id=1, source_target_pairs={{0,1},{2,3},{4,5},{6,7},{8,9},{10,11},{12,13},{14,15},{16,17},{18,... | collective-permute-start | bytes 98312 | tf_op jit(solution)/shard_map/ppermute | solution.py:263
  26.9 3.1 %collective-permute-start.7 = (f32[2,64]{1,0:T(2,128)S(1)}, f32[2,64]{1,0:T(2,128)S(1)}, u32[]{:S(2)}, u32[]{:S(2)}) collective-permute-start(f32[2,64]{1,0:T(2,128)S(1)} %pad_maximum_fusion.34), channel_id=1, source_target_pairs={{0,2},{2,4},{4,6},{6,0},{1,3},{3,5},{5,7},{7,1},{8,10},{10,12},{12... | collective-permute-start | bytes 1544 | tf_op jit(solution)/shard_map/ppermute | solution.py:280
  30.7 2.8 %collective-permute-done.7 = f32[2,64]{1,0:T(2,128)S(1)} collective-permute-done((f32[2,64]{1,0:T(2,128)S(1)}, f32[2,64]{1,0:T(2,128)S(1)}, u32[]{:S(2)}, u32[]{:S(2)}) %collective-permute-start.7) | collective-permute-done | bytes 544 | tf_op jit(solution)/shard_map/ppermute | solution.py:280
  34.7 3.4 %collective-permute-done.8 = f32[4,64]{1,0:T(4,128)S(1)} collective-permute-done((f32[4,64]{1,0:T(4,128)S(1)}, f32[4,64]{1,0:T(4,128)S(1)}, u32[]{:S(2)}, u32[]{:S(2)}) %collective-permute-start.8) | collective-permute-done | bytes 1056 | tf_op jit(solution)/shard_map/ppermute | solution.py:280
  38.1 1.8 %collective-permute-start.9 = (f32[8,64]{1,0:T(8,128)S(1)}, f32[8,64]{1,0:T(8,128)S(1)}, u32[]{:S(2)}, u32[]{:S(2)}) collective-permute-start(f32[8,64]{1,0:T(8,128)S(1)} %pad_maximum_fusion.32), channel_id=1, source_target_pairs={{0,8},{8,16},{16,24},{24,0},{1,9},{9,17},{17,25},{25,1},{2,10},{10... | collective-permute-start | bytes 6152 | tf_op jit(solution)/shard_map/ppermute | solution.py:280
  39.9 2.8 %collective-permute-done.9 = f32[8,64]{1,0:T(8,128)S(1)} collective-permute-done((f32[8,64]{1,0:T(8,128)S(1)}, f32[8,64]{1,0:T(8,128)S(1)}, u32[]{:S(2)}, u32[]{:S(2)}) %collective-permute-start.9) | collective-permute-done | bytes 2080 | tf_op jit(solution)/shard_map/ppermute | solution.py:280
  42.7 1.8 %collective-permute-start.10 = (f32[16,64]{1,0:T(8,128)S(1)}, f32[16,64]{1,0:T(8,128)S(1)}, u32[]{:S(2)}, u32[]{:S(2)}) collective-permute-start(f32[16,64]{1,0:T(8,128)S(1)} %concatenate.226), channel_id=1, source_target_pairs={{0,16},{8,24},{16,0},{24,8},{1,17},{9,25},{17,1},{25,9},{2,18},{10... | collective-permute-start | bytes 12296 | tf_op jit(solution)/shard_map/ppermute | solution.py:280
  44.5 1.9 %collective-permute-done.10 = f32[16,64]{1,0:T(8,128)S(1)} collective-permute-done((f32[16,64]{1,0:T(8,128)S(1)}, f32[16,64]{1,0:T(8,128)S(1)}, u32[]{:S(2)}, u32[]{:S(2)}) %collective-permute-start.10) | collective-permute-done | bytes 4128 | tf_op jit(solution)/shard_map/ppermute | solution.py:280
  48.7 4.5 %collective-permute-start.13 = (f32[80,128]{1,0:T(8,128)S(1)}, f32[80,128]{1,0:T(8,128)S(1)}, u32[]{:S(2)}, u32[]{:S(2)}) collective-permute-start(f32[80,128]{1,0:T(8,128)S(1)} %reshape.386), channel_id=1, source_target_pairs={{0,2},{2,4},{4,6},{1,3},{3,5},{5,7},{8,10},{10,12},{12,14},{9,11},... | collective-permute-start | bytes 122888 | tf_op jit(solution)/shard_map/ppermute | solution.py:263
  55.3 4.6 %collective-permute-start.2 = (f32[280,64]{1,0:T(8,128)S(1)}, f32[280,64]{1,0:T(8,128)S(1)}, u32[]{:S(2)}, u32[]{:S(2)}) collective-permute-start(f32[280,64]{1,0:T(8,128)S(1)} %get-tuple-element.146), channel_id=1, source_target_pairs={{0,2},{2,4},{4,6},{1,3},{3,5},{5,7},{8,10},{10,12},{12,14},{9,11},... | collective-permute-start | bytes 215048 | tf_op jit(solution)/shard_map/ppermute | solution.py:263
  61.3 4.5 %collective-permute-start.15 = (f32[100,128]{1,0:T(8,128)S(1)}, f32[100,128]{1,0:T(8,128)S(1)}, u32[]{:S(2)}, u32[]{:S(2)}) collective-permute-start(f32[100,128]{1,0:T(8,128)S(1)} %reshape.390), channel_id=1, source_target_pairs={{0,8},{8,16},{16,24},{1,9},{9,17},{17,25},{2,10},{10,18},{18,26},{... | collective-permute-start | bytes 153608 | tf_op jit(solution)/shard_map/ppermute | solution.py:263
  68.1 4.7 %collective-permute-start.4 = (f32[488,64]{1,0:T(8,128)S(1)}, f32[488,64]{1,0:T(8,128)S(1)}, u32[]{:S(2)}, u32[]{:S(2)}) collective-permute-start(f32[488,64]{1,0:T(8,128)S(1)} %get-tuple-element.143), channel_id=1, source_target_pairs={{0,8},{8,16},{16,24},{1,9},{9,17},{17,25},{2,10},{10,18},{18,26},{... | collective-permute-start | bytes 374792 | tf_op jit(solution)/shard_map/ppermute | solution.py:263
  73.2 8.4 %shard_map.145 = f32[128,32]{1,0:T(8,128)S(1)} custom-call(f32[10,10,10,128]{3,2,1,0:T(8,128)S(1)} %pad_maximum_fusion.padded), custom_call_target="tpu_custom_call" | custom-call | flops 8589934592 | bytes 1048576 | tf_op jit(solution)/shard_map/pallas_call | solution.py:216
  81.6 8.4 %shard_map.144 = f32[128,32]{1,0:T(8,128)S(1)} custom-call(f32[10,10,10,128]{3,2,1,0:T(8,128)S(1)} %pad_maximum_fusion.padded), custom_call_target="tpu_custom_call" | custom-call | flops 8589934592 | bytes 1048576 | tf_op jit(solution)/shard_map/pallas_call | solution.py:216
  90.0 8.4 %shard_map.143 = f32[128,32]{1,0:T(8,128)S(1)} custom-call(f32[10,10,10,128]{3,2,1,0:T(8,128)S(1)} %pad_maximum_fusion.padded), custom_call_target="tpu_custom_call" | custom-call | flops 8589934592 | bytes 1048576 | tf_op jit(solution)/shard_map/pallas_call | solution.py:216
  98.4 8.4 %shard_map.142 = f32[128,32]{1,0:T(8,128)S(1)} custom-call(f32[10,10,10,128]{3,2,1,0:T(8,128)S(1)} %pad_maximum_fusion.padded), custom_call_target="tpu_custom_call" | custom-call | flops 8589934592 | bytes 1048576 | tf_op jit(solution)/shard_map/pallas_call | solution.py:216
  119.0 5.1 %stack.116.windows = f32[8,8,16,384]{3,2,1,0:T(8,128)S(1)} concatenate(f32[8,8,1,384]{3,2,1,0:T(1,128)S(1)} %copy.121, f32[8,8,1,384]{3,2,1,0:T(1,128)S(1)} %copy.122, f32[8,8,1,384]{3,2,1,0:T(1,128)S(1)} %copy.123, f32[8,8,1,384]{3,2,1,0:T(1,128)S(1)} %copy.124, f32[8,8,1,384]{3,2,1,0:T(1,128)S(1)} %copy.125, f32[8,8,1,384]{3,2,1,0:T(1,128)} %copy.126, f32[8,8,1,384]{3,2,1,0:T(1,128)} %copy.127, ...), dimensions={2} | concatenate | bytes 3145728 | tf_op jit(solution)/shard_map/stack | solution.py:348
  124.1 2.4 %copy-done = bf16[7,7,384,128]{3,2,1,0:T(8,128)(2,1)S(1)} copy-done((bf16[7,7,384,128]{3,2,1,0:T(8,128)(2,1)S(1)}, bf16[7,7,384,128]{3,2,1,0:T(8,128)(2,1)}, u32[]{:S(2)}) %copy-start) | copy-done | bytes 4816920
  126.5 2.4 %copy-done.1 = bf16[7,7,384,128]{3,2,1,0:T(8,128)(2,1)S(1)} copy-done((bf16[7,7,384,128]{3,2,1,0:T(8,128)(2,1)S(1)}, bf16[7,7,384,128]{3,2,1,0:T(8,128)(2,1)}, u32[]{:S(2)}) %copy-start.1) | copy-done | bytes 4816920
  128.9 14.6 %shard_map.141 = f32[512,32]{1,0:T(8,128)S(1)} custom-call(f32[8,8,16,384]{3,2,1,0:T(8,128)S(1)} %stack.116.windows, f32[6,6,16,384]{3,2,1,0:T(8,128)S(1)} %stack.127.small, bf16[7,7,384,128]{3,2,1,0:T(8,128)(2,1)S(1)} %copy-done, bf16[7,7,384,128]{3,2,1,0:T(8,128)(2,1)S(1)} %copy-done.1, f32[128,128]{1,0:T(8,128)S(1)} %copy-done.6, ...), custom_call_target="tpu_custom_call" | custom-call | flops 8589934592 | bytes 1048576 | tf_op jit(solution)/shard_map/pallas_call | solution.py:216
  (195 shorter events, 33.6 us)
Async XLA Ops:
  0.6 45.8 %copy-start.11 = (f32[64,64]{1,0:T(8,128)S(1)}, f32[64,64]{1,0:T(8,128)}, u32[]{:S(2)}) copy-start(f32[64,64]{1,0:T(8,128)} %constant.213.clone) | copy-start | bytes 49156
  0.6 45.8 %copy-start.12 = (f32[64,64]{1,0:T(8,128)S(1)}, f32[64,64]{1,0:T(8,128)}, u32[]{:S(2)}) copy-start(f32[64,64]{1,0:T(8,128)} %constant.212.clone) | copy-start | bytes 49156
  0.7 45.8 %copy-start.13 = (f32[64,64]{1,0:T(8,128)S(1)}, f32[64,64]{1,0:T(8,128)}, u32[]{:S(2)}) copy-start(f32[64,64]{1,0:T(8,128)} %constant.211.clone) | copy-start | bytes 49156
  0.7 46.5 %copy-start.10 = (f32[64,64]{1,0:T(8,128)S(1)}, f32[64,64]{1,0:T(8,128)}, u32[]{:S(2)}) copy-start(f32[64,64]{1,0:T(8,128)} %constant.214.clone) | copy-start | bytes 49156
  0.7 15.3 %copy-start.8 = (f32[8,8,8,128]{3,2,1,0:T(8,128)S(1)}, f32[8,8,8,128]{3,2,1,0:T(8,128)}, u32[]{:S(2)}) copy-start(f32[8,8,8,128]{3,2,1,0:T(8,128)} %param.23) | copy-start | bytes 786436
  11.6 41.7 %collective-permute-start.1 = (f32[168,64]{1,0:T(8,128)S(1)}, f32[168,64]{1,0:T(8,128)S(1)}, u32[]{:S(2)}, u32[]{:S(2)}) collective-permute-start(f32[168,64]{1,0:T(8,128)S(1)} %get-tuple-element.149), channel_id=1, source_target_pairs={{1,0},{3,2},{5,4},{7,6},{9,8},{11,10},{13,12},{15,14},{17,16},{19,... | collective-permute-start | bytes 129032 | tf_op jit(solution)/shard_map/ppermute | solution.py:264
  12.9 40.4 %collective-permute-start = (f32[168,64]{1,0:T(8,128)S(1)}, f32[168,64]{1,0:T(8,128)S(1)}, u32[]{:S(2)}, u32[]{:S(2)}) collective-permute-start(f32[168,64]{1,0:T(8,128)S(1)} %get-tuple-element.148), channel_id=1, source_target_pairs={{0,1},{2,3},{4,5},{6,7},{8,9},{10,11},{12,13},{14,15},{16,17},{18,... | collective-permute-start | bytes 129032 | tf_op jit(solution)/shard_map/ppermute | solution.py:263
  15.9 10.9 %collective-permute-start.6 = (f32[1,64]{1,0:T(1,128)S(1)}, f32[1,64]{1,0:T(1,128)S(1)}, u32[]{:S(2)}, u32[]{:S(2)}) collective-permute-start(f32[1,64]{1,0:T(1,128)S(1)} %slice.379), channel_id=1, source_target_pairs={{0,1},{1,0},{2,3},{3,2},{4,5},{5,4},{6,7},{7,6},{8,9},{9,8},{10,11... | collective-permute-start | bytes 776 | tf_op jit(solution)/shard_map/ppermute | solution.py:280
  16.2 31.0 %collective-permute-start.12 = (f32[64,128]{1,0:T(8,128)S(1)}, f32[64,128]{1,0:T(8,128)S(1)}, u32[]{:S(2)}, u32[]{:S(2)}) collective-permute-start(f32[64,128]{1,0:T(8,128)S(1)} %bitcast.156), channel_id=1, source_target_pairs={{1,0},{3,2},{5,4},{7,6},{9,8},{11,10},{13,12},{15,14},{17,16},{19,... | collective-permute-start | bytes 98312 | tf_op jit(solution)/shard_map/ppermute | solution.py:264
  17.5 29.7 %collective-permute-start.11 = (f32[64,128]{1,0:T(8,128)S(1)}, f32[64,128]{1,0:T(8,128)S(1)}, u32[]{:S(2)}, u32[]{:S(2)}) collective-permute-start(f32[64,128]{1,0:T(8,128)S(1)} %bitcast.155), channel_id=1, source_target_pairs={{0,1},{2,3},{4,5},{6,7},{8,9},{10,11},{12,13},{14,15},{16,17},{18,... | collective-permute-start | bytes 98312 | tf_op jit(solution)/shard_map/ppermute | solution.py:263
  26.9 6.6 %collective-permute-start.7 = (f32[2,64]{1,0:T(2,128)S(1)}, f32[2,64]{1,0:T(2,128)S(1)}, u32[]{:S(2)}, u32[]{:S(2)}) collective-permute-start(f32[2,64]{1,0:T(2,128)S(1)} %pad_maximum_fusion.34), channel_id=1, source_target_pairs={{0,2},{2,4},{4,6},{6,0},{1,3},{3,5},{5,7},{7,1},{8,10},{10,12},{12... | collective-permute-start | bytes 1544 | tf_op jit(solution)/shard_map/ppermute | solution.py:280
  33.5 4.5 %collective-permute-start.8 = (f32[4,64]{1,0:T(4,128)S(1)}, f32[4,64]{1,0:T(4,128)S(1)}, u32[]{:S(2)}, u32[]{:S(2)}) collective-permute-start(f32[4,64]{1,0:T(4,128)S(1)} %pad_maximum_fusion.33), channel_id=1, source_target_pairs={{0,4},{2,6},{4,0},{6,2},{1,5},{3,7},{5,1},{7,3},{8,12},{10,14},{12... | collective-permute-start | bytes 3080 | tf_op jit(solution)/shard_map/ppermute | solution.py:280
  38.1 4.6 %collective-permute-start.9 = (f32[8,64]{1,0:T(8,128)S(1)}, f32[8,64]{1,0:T(8,128)S(1)}, u32[]{:S(2)}, u32[]{:S(2)}) collective-permute-start(f32[8,64]{1,0:T(8,128)S(1)} %pad_maximum_fusion.32), channel_id=1, source_target_pairs={{0,8},{8,16},{16,24},{24,0},{1,9},{9,17},{17,25},{25,1},{2,10},{10... | collective-permute-start | bytes 6152 | tf_op jit(solution)/shard_map/ppermute | solution.py:280
  42.7 3.7 %collective-permute-start.10 = (f32[16,64]{1,0:T(8,128)S(1)}, f32[16,64]{1,0:T(8,128)S(1)}, u32[]{:S(2)}, u32[]{:S(2)}) collective-permute-start(f32[16,64]{1,0:T(8,128)S(1)} %concatenate.226), channel_id=1, source_target_pairs={{0,16},{8,24},{16,0},{24,8},{1,17},{9,25},{17,1},{25,9},{2,18},{10... | collective-permute-start | bytes 12296 | tf_op jit(solution)/shard_map/ppermute | solution.py:280
  47.4 12.4 %collective-permute-start.14 = (f32[80,128]{1,0:T(8,128)S(1)}, f32[80,128]{1,0:T(8,128)S(1)}, u32[]{:S(2)}, u32[]{:S(2)}) collective-permute-start(f32[80,128]{1,0:T(8,128)S(1)} %reshape.388), channel_id=1, source_target_pairs={{2,0},{4,2},{6,4},{3,1},{5,3},{7,5},{10,8},{12,10},{14,12},{11,9},... | collective-permute-start | bytes 122888 | tf_op jit(solution)/shard_map/ppermute | solution.py:264
  48.7 11.1 %collective-permute-start.13 = (f32[80,128]{1,0:T(8,128)S(1)}, f32[80,128]{1,0:T(8,128)S(1)}, u32[]{:S(2)}, u32[]{:S(2)}) collective-permute-start(f32[80,128]{1,0:T(8,128)S(1)} %reshape.386), channel_id=1, source_target_pairs={{0,2},{2,4},{4,6},{1,3},{3,5},{5,7},{8,10},{10,12},{12,14},{9,11},... | collective-permute-start | bytes 122888 | tf_op jit(solution)/shard_map/ppermute | solution.py:263
  54.0 11.9 %collective-permute-start.3 = (f32[280,64]{1,0:T(8,128)S(1)}, f32[280,64]{1,0:T(8,128)S(1)}, u32[]{:S(2)}, u32[]{:S(2)}) collective-permute-start(f32[280,64]{1,0:T(8,128)S(1)} %get-tuple-element.147), channel_id=1, source_target_pairs={{2,0},{4,2},{6,4},{3,1},{5,3},{7,5},{10,8},{12,10},{14,12},{11,9},... | collective-permute-start | bytes 215048 | tf_op jit(solution)/shard_map/ppermute | solution.py:264
  55.3 10.6 %collective-permute-start.2 = (f32[280,64]{1,0:T(8,128)S(1)}, f32[280,64]{1,0:T(8,128)S(1)}, u32[]{:S(2)}, u32[]{:S(2)}) collective-permute-start(f32[280,64]{1,0:T(8,128)S(1)} %get-tuple-element.146), channel_id=1, source_target_pairs={{0,2},{2,4},{4,6},{1,3},{3,5},{5,7},{8,10},{10,12},{12,14},{9,11},... | collective-permute-start | bytes 215048 | tf_op jit(solution)/shard_map/ppermute | solution.py:263
  60.0 12.9 %collective-permute-start.16 = (f32[100,128]{1,0:T(8,128)S(1)}, f32[100,128]{1,0:T(8,128)S(1)}, u32[]{:S(2)}, u32[]{:S(2)}) collective-permute-start(f32[100,128]{1,0:T(8,128)S(1)} %reshape.392), channel_id=1, source_target_pairs={{8,0},{16,8},{24,16},{9,1},{17,9},{25,17},{10,2},{18,10},{26,18},{... | collective-permute-start | bytes 153608 | tf_op jit(solution)/shard_map/ppermute | solution.py:264
  61.3 11.6 %collective-permute-start.15 = (f32[100,128]{1,0:T(8,128)S(1)}, f32[100,128]{1,0:T(8,128)S(1)}, u32[]{:S(2)}, u32[]{:S(2)}) collective-permute-start(f32[100,128]{1,0:T(8,128)S(1)} %reshape.390), channel_id=1, source_target_pairs={{0,8},{8,16},{16,24},{1,9},{9,17},{17,25},{2,10},{10,18},{18,26},{... | collective-permute-start | bytes 153608 | tf_op jit(solution)/shard_map/ppermute | solution.py:263
  66.8 40.7 %collective-permute-start.5 = (f32[488,64]{1,0:T(8,128)S(1)}, f32[488,64]{1,0:T(8,128)S(1)}, u32[]{:S(2)}, u32[]{:S(2)}) collective-permute-start(f32[488,64]{1,0:T(8,128)S(1)} %get-tuple-element.142), channel_id=1, source_target_pairs={{8,0},{16,8},{24,16},{9,1},{17,9},{25,17},{10,2},{18,10},{26,18},{... | collective-permute-start | bytes 374792 | tf_op jit(solution)/shard_map/ppermute | solution.py:264
  68.1 39.6 %collective-permute-start.4 = (f32[488,64]{1,0:T(8,128)S(1)}, f32[488,64]{1,0:T(8,128)S(1)}, u32[]{:S(2)}, u32[]{:S(2)}) collective-permute-start(f32[488,64]{1,0:T(8,128)S(1)} %get-tuple-element.143), channel_id=1, source_target_pairs={{0,8},{8,16},{16,24},{1,9},{9,17},{17,25},{2,10},{10,18},{18,26},{... | collective-permute-start | bytes 374792 | tf_op jit(solution)/shard_map/ppermute | solution.py:263
  113.0 11.1 %copy-start.6 = (f32[128,128]{1,0:T(8,128)S(1)}, f32[128,128]{1,0:T(8,128)}, u32[]{:S(2)}) copy-start(f32[128,128]{1,0:T(8,128)} %constant.217.clone.pair_fit) | copy-start | bytes 196612
  128.9 15.1 %copy-start.9 = (f32[8,8,256]{2,1,0:T(8,128)S(1)}, f32[8,8,256]{2,1,0:T(8,128)}, u32[]{:S(2)}) copy-start(f32[8,8,256]{2,1,0:T(8,128)} %reshape.394) | copy-start | bytes 196612
  (7 other events, 29.6 us)

commit v3 on v2

--- a/solution.py
+++ b/solution.py
@@ -157,9 +157,55 @@
 
 
 def downward_kernel(
-    windows, small, high, low, pair_fit, down, top_local, part, spread, out, total, turned, local
+    leaf_cells,
+    mid_cells,
+    coarse_cells,
+    high,
+    low,
+    pair_fit,
+    down,
+    top_local,
+    part,
+    spread,
+    out,
+    total,
+    turned,
+    local,
+    windows,
+    small,
 ):
     total[...] = jnp.zeros_like(total)
+
+    def window_turn(number, carry):
+        ux = number // 8
+        uy = number % 8
+        row = 0
+        for cz in range(2):
+            for gx in range(2):
+                for gy in range(2):
+                    line = leaf_cells[pl.ds((ux + 4 * gx) * 12 + uy + 4 * gy, 1), :]
+                    for start in (2 * cz * Q, (4 + 2 * cz) * Q):
+                        windows[ux, uy, row : row + 1, :] = line[:, start : start + 6 * Q]
+                        row += 1
+        return carry
+
+    lax.fori_loop(0, 64, window_turn, 0)
+
+    def small_turn(number, carry):
+        sx = number // 6
+        sy = number % 6
+        row = 0
+        for gx in range(2):
+            for gy in range(2):
+                line = mid_cells[pl.ds((sx + 2 * gx) * 8 + sy + 2 * gy, 1), :]
+                for start in (0, 2 * Q):
+                    small[sx, sy, row : row + 1, :] = line[:, start : start + 6 * Q]
+                    row += 1
+        own = coarse_cells[pl.ds(number, 1), :]
+        small[sx, sy, 8:16, :] = jnp.broadcast_to(own, (8, 6 * Q))
+        return carry
+
+    lax.fori_loop(0, 36, small_turn, 0)
 
     def source_turn(number, carry):
         sx = number // 6
@@ -212,12 +258,12 @@
         out[pl.ds(128 * block, 128), :] = value.T
 
 
-def run(kernel, outs, scratch, cost, *args):
+def run(kernel, outs, scratch, cost, limit, *args):
     return pl.pallas_call(
         kernel,
         out_shape=outs,
         scratch_shapes=[pltpu.VMEM(shape, jnp.float32) for shape in scratch],
-        compiler_params=pltpu.CompilerParams(vmem_limit_bytes=40 << 20),
+        compiler_params=pltpu.CompilerParams(vmem_limit_bytes=limit),
         cost_estimate=pl.CostEstimate(flops=cost, bytes_accessed=1 << 20, transcendentals=0),
     )(*args)
 
@@ -321,6 +367,7 @@
         (single(512, Q), single(64, Q), single(8, Q), single(8, Q)),
         [(128, 128)],
         1 << 30,
+        8 << 20,
         part,
         spread,
         np.ascontiguousarray(fit.T),
@@ -334,6 +381,7 @@
                 single(128, 32),
                 [(160, 128)],
                 8 << 30,
+                8 << 20,
                 padded_near,
             )
             for start in (0, 2, 4, 6)
@@ -344,36 +392,15 @@
     leaf_cells, mid_cells, coarse_cells = extended(
         [plain(leaf), plain_mid(mid), coarse.reshape(2, 2, 2, Q)], 2
     )
-    leaf_cells = leaf_cells.reshape(12, 12, 12 * Q)
-    windows = jnp.stack(
-        [
-            leaf_cells[4 * gx : 4 * gx + 8, 4 * gy : 4 * gy + 8, Q * start : Q * start + 6 * Q]
-            for cz in range(2)
-            for gx in range(2)
-            for gy in range(2)
-            for start in (2 * cz, 4 + 2 * cz)
-        ],
-        axis=2,
-    )
-    mid_cells = mid_cells.reshape(8, 8, 8 * Q)
-    small = jnp.stack(
-        [
-            mid_cells[2 * gx : 2 * gx + 6, 2 * gy : 2 * gy + 6, 2 * gz * Q : (2 * gz + 6) * Q]
-            for gx in range(2)
-            for gy in range(2)
-            for gz in range(2)
-        ]
-        + [coarse_cells.reshape(6, 6, 6 * Q)]
-        + [jnp.zeros((6, 6, 6 * Q), jnp.float32)] * 7,
-        axis=2,
-    )
     far = run(
         downward_kernel,
         single(512, 32),
-        [(80, 512), (128, 128), (Q, 128)],
+        [(80, 512), (128, 128), (Q, 128), (8, 8, 16, 6 * Q), (6, 6, 16, 6 * Q)],
         8 << 30,
-        windows,
-        small,
+        30 << 20,
+        leaf_cells.reshape(144, 12 * Q),
+        mid_cells.reshape(64, 8 * Q),
+        coarse_cells.reshape(36, 6 * Q),
         high,
         low,
         pair_fit,

time: 146 us -> 128 us (0.88)
  the two profiles are of different devices: /device:TPU:0 before, /device:TPU:12 now
where the time goes in v3:
time: 128 us; the launch traced here: 127 us
  Pallas kernels  56.1 us (44%)
  starting transfers between devices  39.6 us (31%)
  local copies, waits for them, and re-layouts  10.3 us (8%)
  waiting for transfers between devices  9.29 us (7%)
  other arithmetic  8.96 us (7%)
  between operations  2.78 us (2%)
    pallas_call x6, Pallas kernels, run(): pl.pallas_call(kernel, out_shape=outs, scratch_shapes=[pltpu.VMEM(shape,...  56.1 us
    ppermute x6, starting transfers between devices, extended(): after = unpack(lax.ppermute(pack(heads), axis, backward), heads)  16.6 us
    ppermute x6, starting transfers between devices, extended(): before = unpack(lax.ppermute(pack(tails), axis, forward), tails)  16.5 us
    ppermute x5, waiting for transfers between devices, far_local(): arrived = lax.ppermute(gathered[:take], axis, ring)  9.25 us
    ppermute x5, starting transfers between devices, far_local(): arrived = lax.ppermute(gathered[:take], axis, ring)  6.46 us
    unnamed x27, local copies, waits for them, and re-layouts  5.35 us
    another operation x6, other arithmetic  3.79 us
  transfers between devices with their start and end apart: 17, of which 4 were waited for; matrix products, arithmetic and copies ran while one was open for 8% of the time, Pallas kernels for 31%

profile of v3, /device:TPU:12, one launch (start us, length us, event | category | flops | bytes accessed | tf_op | source)
XLA Modules:
  0.0 127.1 jit_solution(11335352811862333331)
XLA Ops:
  4.4 3.0 %collective-permute-start.11 = (f32[64,128]{1,0:T(8,128)S(1)}, f32[64,128]{1,0:T(8,128)S(1)}, u32[]{:S(2)}, u32[]{:S(2)}) collective-permute-start(f32[64,128]{1,0:T(8,128)S(1)} %bitcast.126), channel_id=1, source_target_pairs={{0,1},{2,3},{4,5},{6,7},{8,9},{10,11},{12,13},{14,15},{16,17},{18,... | collective-permute-start | bytes 98312 | tf_op jit(solution)/shard_map/ppermute | solution.py:309
  7.8 5.5 %shard_map.140 = (f32[512,64]{1,0:T(8,128)S(1)}, f32[64,64]{1,0:T(8,128)S(1)}, f32[8,64]{1,0:T(8,128)S(1)}, f32[8,64]{1,0:T(8,128)S(1)}) custom-call(f32[512,128]{1,0:T(8,128)S(1)} %bitcast.62, f32[3,64,128]{2,1,0:T(8,128)S(1)} %copy-done.4, f32[64,64]{1,0:T(8,128)S(1)} %copy-done.6, f32[512,64]{1,0:T(8,128)S(1)} %copy-done.2), custom_call_target="tpu_custom_call" | custom-call | flops 1073741824 | bytes 1048576 | tf_op jit(solution)/shard_map/pallas_call | solution.py:262
  13.7 2.4 %collective-permute-start = (f32[168,64]{1,0:T(8,128)S(1)}, f32[168,64]{1,0:T(8,128)S(1)}, u32[]{:S(2)}, u32[]{:S(2)}) collective-permute-start(f32[168,64]{1,0:T(8,128)S(1)} %get-tuple-element.120), channel_id=1, source_target_pairs={{0,1},{2,3},{4,5},{6,7},{8,9},{10,11},{12,13},{14,15},{16,17},{18,... | collective-permute-start | bytes 129032 | tf_op jit(solution)/shard_map/ppermute | solution.py:309
  23.6 1.6 %collective-permute-start.7 = (f32[2,64]{1,0:T(2,128)S(1)}, f32[2,64]{1,0:T(2,128)S(1)}, u32[]{:S(2)}, u32[]{:S(2)}) collective-permute-start(f32[2,64]{1,0:T(2,128)S(1)} %pad_maximum_fusion.36), channel_id=1, source_target_pairs={{0,2},{2,4},{4,6},{6,0},{1,3},{3,5},{5,7},{7,1},{8,10},{10,12},{12... | collective-permute-start | bytes 1544 | tf_op jit(solution)/shard_map/ppermute | solution.py:326
  27.2 2.7 %collective-permute-start.8 = (f32[4,64]{1,0:T(4,128)S(1)}, f32[4,64]{1,0:T(4,128)S(1)}, u32[]{:S(2)}, u32[]{:S(2)}) collective-permute-start(f32[4,64]{1,0:T(4,128)S(1)} %pad_maximum_fusion.35), channel_id=1, source_target_pairs={{0,4},{2,6},{4,0},{6,2},{1,5},{3,7},{5,1},{7,3},{8,12},{10,14},{12... | collective-permute-start | bytes 3080 | tf_op jit(solution)/shard_map/ppermute | solution.py:326
  30.0 1.8 %collective-permute-done.8 = f32[4,64]{1,0:T(4,128)S(1)} collective-permute-done((f32[4,64]{1,0:T(4,128)S(1)}, f32[4,64]{1,0:T(4,128)S(1)}, u32[]{:S(2)}, u32[]{:S(2)}) %collective-permute-start.8) | collective-permute-done | bytes 1056 | tf_op jit(solution)/shard_map/ppermute | solution.py:326
  31.8 1.5 %collective-permute-start.9 = (f32[8,64]{1,0:T(8,128)S(1)}, f32[8,64]{1,0:T(8,128)S(1)}, u32[]{:S(2)}, u32[]{:S(2)}) collective-permute-start(f32[8,64]{1,0:T(8,128)S(1)} %pad_maximum_fusion.34), channel_id=1, source_target_pairs={{0,8},{8,16},{16,24},{24,0},{1,9},{9,17},{17,25},{25,1},{2,10},{10... | collective-permute-start | bytes 6152 | tf_op jit(solution)/shard_map/ppermute | solution.py:326
  33.3 3.0 %collective-permute-done.9 = f32[8,64]{1,0:T(8,128)S(1)} collective-permute-done((f32[8,64]{1,0:T(8,128)S(1)}, f32[8,64]{1,0:T(8,128)S(1)}, u32[]{:S(2)}, u32[]{:S(2)}) %collective-permute-start.9) | collective-permute-done | bytes 2080 | tf_op jit(solution)/shard_map/ppermute | solution.py:326
  36.9 3.1 %collective-permute-done.10 = f32[16,64]{1,0:T(8,128)S(1)} collective-permute-done((f32[16,64]{1,0:T(8,128)S(1)}, f32[16,64]{1,0:T(8,128)S(1)}, u32[]{:S(2)}, u32[]{:S(2)}) %collective-permute-start.10) | collective-permute-done | bytes 4128 | tf_op jit(solution)/shard_map/ppermute | solution.py:326
  41.1 4.2 %collective-permute-start.14 = (f32[80,128]{1,0:T(8,128)S(1)}, f32[80,128]{1,0:T(8,128)S(1)}, u32[]{:S(2)}, u32[]{:S(2)}) collective-permute-start(f32[80,128]{1,0:T(8,128)S(1)} %reshape.386), channel_id=1, source_target_pairs={{2,0},{4,2},{6,4},{3,1},{5,3},{7,5},{10,8},{12,10},{14,12},{11,9},... | collective-permute-start | bytes 122888 | tf_op jit(solution)/shard_map/ppermute | solution.py:310
  45.3 1.9 %collective-permute-start.13 = (f32[80,128]{1,0:T(8,128)S(1)}, f32[80,128]{1,0:T(8,128)S(1)}, u32[]{:S(2)}, u32[]{:S(2)}) collective-permute-start(f32[80,128]{1,0:T(8,128)S(1)} %reshape.384), channel_id=1, source_target_pairs={{0,2},{2,4},{4,6},{1,3},{3,5},{5,7},{8,10},{10,12},{12,14},{9,11},... | collective-permute-start | bytes 122888 | tf_op jit(solution)/shard_map/ppermute | solution.py:309
  47.5 3.2 %collective-permute-start.2 = (f32[280,64]{1,0:T(8,128)S(1)}, f32[280,64]{1,0:T(8,128)S(1)}, u32[]{:S(2)}, u32[]{:S(2)}) collective-permute-start(f32[280,64]{1,0:T(8,128)S(1)} %get-tuple-element.118), channel_id=1, source_target_pairs={{0,2},{2,4},{4,6},{1,3},{3,5},{5,7},{8,10},{10,12},{12,14},{9,11},... | collective-permute-start | bytes 215048 | tf_op jit(solution)/shard_map/ppermute | solution.py:309
  50.8 2.6 %collective-permute-start.3 = (f32[280,64]{1,0:T(8,128)S(1)}, f32[280,64]{1,0:T(8,128)S(1)}, u32[]{:S(2)}, u32[]{:S(2)}) collective-permute-start(f32[280,64]{1,0:T(8,128)S(1)} %get-tuple-element.119), channel_id=1, source_target_pairs={{2,0},{4,2},{6,4},{3,1},{5,3},{7,5},{10,8},{12,10},{14,12},{11,9},... | collective-permute-start | bytes 215048 | tf_op jit(solution)/shard_map/ppermute | solution.py:310
  54.2 2.4 %collective-permute-start.16 = (f32[100,128]{1,0:T(8,128)}, f32[100,128]{1,0:T(8,128)}, u32[]{:S(2)}, u32[]{:S(2)}) collective-permute-start(f32[100,128]{1,0:T(8,128)} %reshape.390), channel_id=1, source_target_pairs={{8,0},{16,8},{24,16},{9,1},{17,9},{25,17},{10,2},{18,10},{26,18},{... | collective-permute-start | bytes 153608 | tf_op jit(solution)/shard_map/ppermute | solution.py:310
  56.6 4.0 %collective-permute-start.15 = (f32[100,128]{1,0:T(8,128)S(1)}, f32[100,128]{1,0:T(8,128)S(1)}, u32[]{:S(2)}, u32[]{:S(2)}) collective-permute-start(f32[100,128]{1,0:T(8,128)S(1)} %reshape.388), channel_id=1, source_target_pairs={{0,8},{8,16},{16,24},{1,9},{9,17},{17,25},{2,10},{10,18},{18,26},{... | collective-permute-start | bytes 153608 | tf_op jit(solution)/shard_map/ppermute | solution.py:309
  61.1 1.9 %collective-permute-start.4 = (f32[488,64]{1,0:T(8,128)S(1)}, f32[488,64]{1,0:T(8,128)S(1)}, u32[]{:S(2)}, u32[]{:S(2)}) collective-permute-start(f32[488,64]{1,0:T(8,128)S(1)} %get-tuple-element.114), channel_id=1, source_target_pairs={{0,8},{8,16},{16,24},{1,9},{9,17},{17,25},{2,10},{10,18},{18,26},{... | collective-permute-start | bytes 374792 | tf_op jit(solution)/shard_map/ppermute | solution.py:309
  63.0 4.8 %collective-permute-start.5 = (f32[488,64]{1,0:T(8,128)S(1)}, f32[488,64]{1,0:T(8,128)S(1)}, u32[]{:S(2)}, u32[]{:S(2)}) collective-permute-start(f32[488,64]{1,0:T(8,128)S(1)} %get-tuple-element.115), channel_id=1, source_target_pairs={{8,0},{16,8},{24,16},{9,1},{17,9},{25,17},{10,2},{18,10},{26,18},{... | collective-permute-start | bytes 374792 | tf_op jit(solution)/shard_map/ppermute | solution.py:310
  68.9 8.4 %shard_map.145 = f32[128,32]{1,0:T(8,128)S(1)} custom-call(f32[10,10,10,128]{3,2,1,0:T(8,128)S(1)} %pad_maximum_fusion.1.padded), custom_call_target="tpu_custom_call" | custom-call | flops 8589934592 | bytes 1048576 | tf_op jit(solution)/shard_map/pallas_call | solution.py:262
  77.3 8.4 %shard_map.144 = f32[128,32]{1,0:T(8,128)S(1)} custom-call(f32[10,10,10,128]{3,2,1,0:T(8,128)S(1)} %pad_maximum_fusion.1.padded), custom_call_target="tpu_custom_call" | custom-call | flops 8589934592 | bytes 1048576 | tf_op jit(solution)/shard_map/pallas_call | solution.py:262
  85.7 8.4 %shard_map.143 = f32[128,32]{1,0:T(8,128)S(1)} custom-call(f32[10,10,10,128]{3,2,1,0:T(8,128)S(1)} %pad_maximum_fusion.1.padded), custom_call_target="tpu_custom_call" | custom-call | flops 8589934592 | bytes 1048576 | tf_op jit(solution)/shard_map/pallas_call | solution.py:262
  94.1 8.4 %shard_map.142 = f32[128,32]{1,0:T(8,128)S(1)} custom-call(f32[10,10,10,128]{3,2,1,0:T(8,128)S(1)} %pad_maximum_fusion.1.padded), custom_call_target="tpu_custom_call" | custom-call | flops 8589934592 | bytes 1048576 | tf_op jit(solution)/shard_map/pallas_call | solution.py:262
  104.3 2.4 %copy-done = bf16[7,7,384,128]{3,2,1,0:T(8,128)(2,1)S(1)} copy-done((bf16[7,7,384,128]{3,2,1,0:T(8,128)(2,1)S(1)}, bf16[7,7,384,128]{3,2,1,0:T(8,128)(2,1)}, u32[]{:S(2)}) %copy-start) | copy-done | bytes 4816920
  106.6 2.4 %copy-done.1 = bf16[7,7,384,128]{3,2,1,0:T(8,128)(2,1)S(1)} copy-done((bf16[7,7,384,128]{3,2,1,0:T(8,128)(2,1)S(1)}, bf16[7,7,384,128]{3,2,1,0:T(8,128)(2,1)}, u32[]{:S(2)}) %copy-start.1) | copy-done | bytes 4816920
  109.0 17.0 %shard_map.141 = f32[512,32]{1,0:T(8,128)S(1)} custom-call(f32[144,768]{1,0:T(8,128)S(1)} %reshape.371.leaf_cells, f32[64,512]{1,0:T(8,128)S(1)} %reshape.374.mid_cells, f32[36,384]{1,0:T(8,128)S(1)} %reshape.377.coarse_cells, bf16[7,7,384,128]{3,2,1,0:T(8,128)(2,1)S(1)} %copy-done.1, bf16[7,7,384,128]{3,2,1,0:T(8,128)(2,1)S(1)} %copy-done, ...), custom_call_target="tpu_custom_call" | custom-call | flops 8589934592 | bytes 1048576 | tf_op jit(solution)/shard_map/pallas_call | solution.py:262
  (151 shorter events, 19.2 us)
Async XLA Ops:
  0.6 7.1 %copy-start.2 = (f32[512,64]{1,0:T(8,128)S(1)}, f32[512,64]{1,0:T(8,128)}, u32[]{:S(2)}) copy-start(f32[512,64]{1,0:T(8,128)} %constant.207.clone.up) | copy-start | bytes 393220
  0.6 7.1 %copy-start.4 = (f32[3,64,128]{2,1,0:T(8,128)S(1)}, f32[3,64,128]{2,1,0:T(8,128)}, u32[]{:S(2)}) copy-start(f32[3,64,128]{2,1,0:T(8,128)} %constant.205.clone.spread) | copy-start | bytes 294916
  3.1 37.8 %collective-permute-start.12 = (f32[64,128]{1,0:T(8,128)S(1)}, f32[64,128]{1,0:T(8,128)S(1)}, u32[]{:S(2)}, u32[]{:S(2)}) collective-permute-start(f32[64,128]{1,0:T(8,128)S(1)} %bitcast.127), channel_id=1, source_target_pairs={{1,0},{3,2},{5,4},{7,6},{9,8},{11,10},{13,12},{15,14},{17,16},{19,... | collective-permute-start | bytes 98312 | tf_op jit(solution)/shard_map/ppermute | solution.py:310
  4.4 36.5 %collective-permute-start.11 = (f32[64,128]{1,0:T(8,128)S(1)}, f32[64,128]{1,0:T(8,128)S(1)}, u32[]{:S(2)}, u32[]{:S(2)}) collective-permute-start(f32[64,128]{1,0:T(8,128)S(1)} %bitcast.126), channel_id=1, source_target_pairs={{0,1},{2,3},{4,5},{6,7},{8,9},{10,11},{12,13},{14,15},{16,17},{18,... | collective-permute-start | bytes 98312 | tf_op jit(solution)/shard_map/ppermute | solution.py:309
  13.3 26.8 %copy-start.10 = (f32[64,64]{1,0:T(8,128)S(1)}, f32[64,64]{1,0:T(8,128)}, u32[]{:S(2)}) copy-start(f32[64,64]{1,0:T(8,128)} %constant.210.clone) | copy-start | bytes 49156
  13.3 26.8 %copy-start.11 = (f32[64,64]{1,0:T(8,128)S(1)}, f32[64,64]{1,0:T(8,128)}, u32[]{:S(2)}) copy-start(f32[64,64]{1,0:T(8,128)} %constant.209.clone) | copy-start | bytes 49156
  13.3 26.8 %copy-start.12 = (f32[64,64]{1,0:T(8,128)S(1)}, f32[64,64]{1,0:T(8,128)}, u32[]{:S(2)}) copy-start(f32[64,64]{1,0:T(8,128)} %constant.208.clone) | copy-start | bytes 49156
  13.3 27.5 %copy-start.9 = (f32[64,64]{1,0:T(8,128)S(1)}, f32[64,64]{1,0:T(8,128)}, u32[]{:S(2)}) copy-start(f32[64,64]{1,0:T(8,128)} %constant.211.clone) | copy-start | bytes 49156
  13.3 10.3 %collective-permute-start.6 = (f32[1,64]{1,0:T(1,128)S(1)}, f32[1,64]{1,0:T(1,128)S(1)}, u32[]{:S(2)}, u32[]{:S(2)}) collective-permute-start(f32[1,64]{1,0:T(1,128)S(1)} %slice.259), channel_id=1, source_target_pairs={{0,1},{1,0},{2,3},{3,2},{4,5},{5,4},{6,7},{7,6},{8,9},{9,8},{10,11... | collective-permute-start | bytes 776 | tf_op jit(solution)/shard_map/ppermute | solution.py:326
  13.7 33.5 %collective-permute-start = (f32[168,64]{1,0:T(8,128)S(1)}, f32[168,64]{1,0:T(8,128)S(1)}, u32[]{:S(2)}, u32[]{:S(2)}) collective-permute-start(f32[168,64]{1,0:T(8,128)S(1)} %get-tuple-element.120), channel_id=1, source_target_pairs={{0,1},{2,3},{4,5},{6,7},{8,9},{10,11},{12,13},{14,15},{16,17},{18,... | collective-permute-start | bytes 129032 | tf_op jit(solution)/shard_map/ppermute | solution.py:309
  16.1 31.1 %collective-permute-start.1 = (f32[168,64]{1,0:T(8,128)S(1)}, f32[168,64]{1,0:T(8,128)S(1)}, u32[]{:S(2)}, u32[]{:S(2)}) collective-permute-start(f32[168,64]{1,0:T(8,128)S(1)} %get-tuple-element.121), channel_id=1, source_target_pairs={{1,0},{3,2},{5,4},{7,6},{9,8},{11,10},{13,12},{15,14},{17,16},{19,... | collective-permute-start | bytes 129032 | tf_op jit(solution)/shard_map/ppermute | solution.py:310
  23.6 3.6 %collective-permute-start.7 = (f32[2,64]{1,0:T(2,128)S(1)}, f32[2,64]{1,0:T(2,128)S(1)}, u32[]{:S(2)}, u32[]{:S(2)}) collective-permute-start(f32[2,64]{1,0:T(2,128)S(1)} %pad_maximum_fusion.36), channel_id=1, source_target_pairs={{0,2},{2,4},{4,6},{6,0},{1,3},{3,5},{5,7},{7,1},{8,10},{10,12},{12... | collective-permute-start | bytes 1544 | tf_op jit(solution)/shard_map/ppermute | solution.py:326
  27.2 4.5 %collective-permute-start.8 = (f32[4,64]{1,0:T(4,128)S(1)}, f32[4,64]{1,0:T(4,128)S(1)}, u32[]{:S(2)}, u32[]{:S(2)}) collective-permute-start(f32[4,64]{1,0:T(4,128)S(1)} %pad_maximum_fusion.35), channel_id=1, source_target_pairs={{0,4},{2,6},{4,0},{6,2},{1,5},{3,7},{5,1},{7,3},{8,12},{10,14},{12... | collective-permute-start | bytes 3080 | tf_op jit(solution)/shard_map/ppermute | solution.py:326
  31.8 4.6 %collective-permute-start.9 = (f32[8,64]{1,0:T(8,128)S(1)}, f32[8,64]{1,0:T(8,128)S(1)}, u32[]{:S(2)}, u32[]{:S(2)}) collective-permute-start(f32[8,64]{1,0:T(8,128)S(1)} %pad_maximum_fusion.34), channel_id=1, source_target_pairs={{0,8},{8,16},{16,24},{24,0},{1,9},{9,17},{17,25},{25,1},{2,10},{10... | collective-permute-start | bytes 6152 | tf_op jit(solution)/shard_map/ppermute | solution.py:326
  36.4 3.7 %collective-permute-start.10 = (f32[16,64]{1,0:T(8,128)S(1)}, f32[16,64]{1,0:T(8,128)S(1)}, u32[]{:S(2)}, u32[]{:S(2)}) collective-permute-start(f32[16,64]{1,0:T(8,128)S(1)} %concatenate.136), channel_id=1, source_target_pairs={{0,16},{8,24},{16,0},{24,8},{1,17},{9,25},{17,1},{25,9},{2,18},{10... | collective-permute-start | bytes 12296 | tf_op jit(solution)/shard_map/ppermute | solution.py:326
  41.1 12.3 %collective-permute-start.14 = (f32[80,128]{1,0:T(8,128)S(1)}, f32[80,128]{1,0:T(8,128)S(1)}, u32[]{:S(2)}, u32[]{:S(2)}) collective-permute-start(f32[80,128]{1,0:T(8,128)S(1)} %reshape.386), channel_id=1, source_target_pairs={{2,0},{4,2},{6,4},{3,1},{5,3},{7,5},{10,8},{12,10},{14,12},{11,9},... | collective-permute-start | bytes 122888 | tf_op jit(solution)/shard_map/ppermute | solution.py:310
  45.3 8.1 %collective-permute-start.13 = (f32[80,128]{1,0:T(8,128)S(1)}, f32[80,128]{1,0:T(8,128)S(1)}, u32[]{:S(2)}, u32[]{:S(2)}) collective-permute-start(f32[80,128]{1,0:T(8,128)S(1)} %reshape.384), channel_id=1, source_target_pairs={{0,2},{2,4},{4,6},{1,3},{3,5},{5,7},{8,10},{10,12},{12,14},{9,11},... | collective-permute-start | bytes 122888 | tf_op jit(solution)/shard_map/ppermute | solution.py:309
  47.5 13.1 %collective-permute-start.2 = (f32[280,64]{1,0:T(8,128)S(1)}, f32[280,64]{1,0:T(8,128)S(1)}, u32[]{:S(2)}, u32[]{:S(2)}) collective-permute-start(f32[280,64]{1,0:T(8,128)S(1)} %get-tuple-element.118), channel_id=1, source_target_pairs={{0,2},{2,4},{4,6},{1,3},{3,5},{5,7},{8,10},{10,12},{12,14},{9,11},... | collective-permute-start | bytes 215048 | tf_op jit(solution)/shard_map/ppermute | solution.py:309
  50.8 9.9 %collective-permute-start.3 = (f32[280,64]{1,0:T(8,128)S(1)}, f32[280,64]{1,0:T(8,128)S(1)}, u32[]{:S(2)}, u32[]{:S(2)}) collective-permute-start(f32[280,64]{1,0:T(8,128)S(1)} %get-tuple-element.119), channel_id=1, source_target_pairs={{2,0},{4,2},{6,4},{3,1},{5,3},{7,5},{10,8},{12,10},{14,12},{11,9},... | collective-permute-start | bytes 215048 | tf_op jit(solution)/shard_map/ppermute | solution.py:310
  54.2 13.6 %collective-permute-start.16 = (f32[100,128]{1,0:T(8,128)}, f32[100,128]{1,0:T(8,128)}, u32[]{:S(2)}, u32[]{:S(2)}) collective-permute-start(f32[100,128]{1,0:T(8,128)} %reshape.390), channel_id=1, source_target_pairs={{8,0},{16,8},{24,16},{9,1},{17,9},{25,17},{10,2},{18,10},{26,18},{... | collective-permute-start | bytes 153608 | tf_op jit(solution)/shard_map/ppermute | solution.py:310
  56.6 12.0 %collective-permute-start.15 = (f32[100,128]{1,0:T(8,128)S(1)}, f32[100,128]{1,0:T(8,128)S(1)}, u32[]{:S(2)}, u32[]{:S(2)}) collective-permute-start(f32[100,128]{1,0:T(8,128)S(1)} %reshape.388), channel_id=1, source_target_pairs={{0,8},{8,16},{16,24},{1,9},{9,17},{17,25},{2,10},{10,18},{18,26},{... | collective-permute-start | bytes 153608 | tf_op jit(solution)/shard_map/ppermute | solution.py:309
  61.1 41.6 %collective-permute-start.4 = (f32[488,64]{1,0:T(8,128)S(1)}, f32[488,64]{1,0:T(8,128)S(1)}, u32[]{:S(2)}, u32[]{:S(2)}) collective-permute-start(f32[488,64]{1,0:T(8,128)S(1)} %get-tuple-element.114), channel_id=1, source_target_pairs={{0,8},{8,16},{16,24},{1,9},{9,17},{17,25},{2,10},{10,18},{18,26},{... | collective-permute-start | bytes 374792 | tf_op jit(solution)/shard_map/ppermute | solution.py:309
  63.0 39.8 %collective-permute-start.5 = (f32[488,64]{1,0:T(8,128)S(1)}, f32[488,64]{1,0:T(8,128)S(1)}, u32[]{:S(2)}, u32[]{:S(2)}) collective-permute-start(f32[488,64]{1,0:T(8,128)S(1)} %get-tuple-element.115), channel_id=1, source_target_pairs={{8,0},{16,8},{24,16},{9,1},{17,9},{25,17},{10,2},{18,10},{26,18},{... | collective-permute-start | bytes 374792 | tf_op jit(solution)/shard_map/ppermute | solution.py:310
  102.7 23.8 %copy-start.8 = (f32[8,8,256]{2,1,0:T(8,128)}, f32[8,8,256]{2,1,0:T(8,128)S(1)}, u32[]{:S(2)}) copy-start(f32[8,8,256]{2,1,0:T(8,128)S(1)} %reshape.392) | copy-start | bytes 196612
  (6 other events, 20.5 us)
